TPU v7x, 32 devices: a whole 2x2x4 slice. The times are simulated.
32 devices in a mesh: rep: 8 (over z, y), shard: 4 (over x, core).
Axes of the slice: x: 2, y: 2, z: 4, core: 2. Of those that a mesh axis runs over, the one named last changes fastest.
Arguments:
- tokens: bfloat16 [4096, 1024], P(('rep', 'shard')), may hold values from -6 to 6
- cotangent: bfloat16 [4096, 1024], P(('rep', 'shard')), may hold values from -6 to 6
- doc_ids: int32 [4096], P(('rep', 'shard')), may hold values from -1 to 15, as said below
- w_query: bfloat16 [1024, 1024], P('shard'), may hold values from -0.1875 to 0.1875
- w_key: bfloat16 [1024, 512], P('shard'), may hold values from -0.1875 to 0.1875
- w_value: bfloat16 [1024, 512], P('shard'), may hold values from -0.1875 to 0.1875
- w_out: bfloat16 [1024, 1024], P('shard'), may hold values from -0.5 to 0.5
- w_gate: bfloat16 [1024, 4608], P('shard'), may hold values from -0.1875 to 0.1875
- w_up: bfloat16 [1024, 4608], P('shard'), may hold values from -0.1875 to 0.1875
- w_down: bfloat16 [4608, 1024], P('shard'), may hold values from -0.09375 to 0.09375
- gain_attn: bfloat16 [1024], P('shard'), may hold values from 0.5 to 1.5
- gain_ffn: bfloat16 [1024], P('shard'), may hold values from 0.5 to 1.5
- gain_query: bfloat16 [64], P('shard'), may hold values from 0.5 to 1.5
- gain_key: bfloat16 [64], P('shard'), may hold values from 0.5 to 1.5
Outputs:
- block_out: bfloat16 [4096, 1024], P(('rep', 'shard'))
- grad_tokens: float32 [4096, 1024], P(('rep', 'shard'))
- grad_w_query: float32 [1024, 1024], P('shard')
- grad_w_key: float32 [1024, 512], P('shard')
- grad_w_value: float32 [1024, 512], P('shard')
- grad_w_out: float32 [1024, 1024], P('shard')
- grad_w_gate: float32 [1024, 4608], P('shard')
- grad_w_up: float32 [1024, 4608], P('shard')
- grad_w_down: float32 [4608, 1024], P('shard')
- grad_gain_attn: float32 [1024], P('shard')
- grad_gain_ffn: float32 [1024], P('shard')
- grad_gain_query: float32 [64], P('shard')
- grad_gain_key: float32 [64], P('shard')
Inputs may be any that keep to these rules, and one draw needn't show every extreme that they name: `doc_ids`: each device's 128 slots hold its sequences one after another, numbered from 0 upward without gaps, followed by its empty slots marked -1; at least one device has no empty slot and holds 16 sequences.
All inputs are finite; a program needn't handle non-finite values.
Results may differ from a plain program's by a relative error of at most 0.02.
Values may be sent and summed in bfloat16 or wider, within the bound.
A program may use at most 192 MiB of HBM per device.

v0:
```python
import functools
import math

import jax
import jax.numpy as jnp
from jax import lax
from jax.experimental import pallas as pl
from jax.experimental.pallas import tpu as pltpu
from jax.sharding import PartitionSpec as P

MESH = pl.DeviceIdType.MESH

QH = 16
KVH = 8
HEAD_DIM = 64


NORM_EPSILON = 1e-05
ROPE_BASE = 1000000.0


def matmul(left, right):
    return jnp.dot(left, right, preferred_element_type=jnp.float32)


def matmul_t(left, right):
    return lax.dot_general(left, right, (((1,), (1,)), ((), ())), preferred_element_type=jnp.float32)


def norm_rows(values, gain_vec):
    inv_rms = lax.rsqrt(jnp.mean(values * values, axis=-1, keepdims=True) + NORM_EPSILON)
    normed = values * inv_rms
    return (normed * gain_vec.astype(jnp.float32), normed, inv_rms)


def norm_back(grad_out, normed, inv_rms, gain_vec):
    scaled = grad_out * gain_vec.astype(jnp.float32)
    grad_in = inv_rms * (scaled - normed * jnp.mean(scaled * normed, axis=-1, keepdims=True))
    lead_axes = tuple(range(grad_out.ndim - 1))
    return (grad_in, jnp.sum(grad_out * normed, axis=lead_axes))


def doc_tables(doc_rows):
    block_len = doc_rows.shape[-1]
    row_index = jnp.arange(block_len)[:, None]
    col_index = jnp.arange(block_len)[None, :]
    same_doc = doc_rows[:, :, None] == doc_rows[:, None, :]
    allowed = same_doc & (row_index >= col_index)[None]
    earlier = same_doc & (row_index > col_index)[None]
    positions = jnp.sum(earlier.astype(jnp.int32), axis=2)
    return (allowed, positions)


def rope_tables(positions, head_dim):
    half_dim = head_dim // 2
    inv_freq = jnp.exp(
        jnp.arange(half_dim).astype(jnp.float32) * (-2.0 * math.log(ROPE_BASE) / head_dim)
    )
    angles = positions.astype(jnp.float32)[:, :, None, None] * inv_freq
    return (jnp.cos(angles), jnp.sin(angles))


def rotate(values, cos_tab, sin_tab):
    half_dim = values.shape[-1] // 2
    part_one = values[..., :half_dim]
    part_two = values[..., half_dim:]
    return jnp.concatenate(
        [part_one * cos_tab - part_two * sin_tab, part_two * cos_tab + part_one * sin_tab], axis=-1
    )


def rotate_back(values, cos_tab, sin_tab):
    half_dim = values.shape[-1] // 2
    part_one = values[..., :half_dim]
    part_two = values[..., half_dim:]
    return jnp.concatenate(
        [part_one * cos_tab + part_two * sin_tab, part_two * cos_tab - part_one * sin_tab], axis=-1
    )


def attn_probs_of(query_bf, key_bf, key_mask, log_total, score_scale):
    scores = (
        jnp.einsum("gqkrd,gskd->gkrqs", query_bf, key_bf, preferred_element_type=jnp.float32)
        * score_scale
    )
    if log_total is None:
        log_total = jnp.log(
            jnp.sum(jnp.where(key_mask, jnp.exp(scores), 0.0), axis=-1, keepdims=True)
        )
    return (jnp.where(key_mask, jnp.exp(scores - log_total), 0.0), log_total)


def bit_count(size):
    return size.bit_length() - 1


def gather_kernel(cfg, *refs):
    items, n_in, n_out = cfg["items"], cfg["n_in"], cfg["n_out"]
    ins, outs = refs[:n_in], refs[n_in : n_in + n_out]
    gain_in, gain_out = ins[-1], outs[-1]
    send_sem, recv_sem, own_sem, gs_sem, gr_sem, go_sem = refs[n_in + n_out :]
    me_s, me_r = lax.axis_index("shard"), lax.axis_index("rep")
    core, y, z = me_s & 1, me_r & 1, (me_r >> 1) & 1
    peers = [{"shard": me_s ^ 1}, {"shard": me_s ^ 2}, {"rep": me_r ^ 1}, {"rep": me_r ^ 2}]
    to_core, to_x, to_y, to_z = peers
    barrier = pltpu.get_barrier_semaphore()
    for p in peers:
        pl.semaphore_signal(barrier, inc=1, device_id=p, device_id_type=MESH)
    pl.semaphore_wait(barrier, len(peers))

    other = me_s ^ 2
    mine = z * 2 + y
    from_y, from_z, diag = mine ^ 1, mine ^ 2, mine ^ 3

    def place(n, shard, row, size):
        it = items[n]
        return outs[it["out"]].at[shard, pl.ds(it["row"] + row, size), pl.ds(it["dst"], it["cols"])]

    def fresh(n, row, size):
        it = items[n]
        return ins[it["in"]].at[pl.ds(it["row"] + row, size), pl.ds(it["src"], it["cols"])]

    def send(n, i, src, dst, to):
        return pltpu.make_async_remote_copy(
            src_ref=src, dst_ref=dst, send_sem=send_sem.at[n, i], recv_sem=recv_sem.at[n, i],
            device_id=to, device_id_type=MESH)

    def relay(n, i, row, size, to):
        ref = place(n, other, row, size)
        return send(n, i, ref, ref, to)

    def copies(n):
        it = items[n]
        rows, quarter = it["rows"], it["rows"] // 4
        dx, dy, dz = it["parts"]
        at = lambda q: pl.multiple_of(q * quarter, quarter)
        whole = lambda i, row, size, to: send(n, i, fresh(n, row, size), place(n, me_s, row, size), to)
        return dict(
            x=whole(0, at(mine), quarter, to_x),
            xd=whole(1, at(diag), dx, to_x),
            own=whole(2, 0, rows, to_core),
            y=relay(n, 3, at(mine), quarter, to_y),
            z=relay(n, 4, at(mine), quarter, to_z),
            c0=relay(n, 5, at(mine), quarter, to_core),
            fz=relay(n, 6, at(from_y) + dx + dy, dz, to_z),
            c1=relay(n, 7, at(from_y), quarter, to_core),
            fy=relay(n, 8, at(from_z) + dx, dy, to_y),
            c2=relay(n, 9, at(from_z), quarter, to_core),
            c3=relay(n, 10, at(diag), quarter, to_core),
            keep=pltpu.make_async_copy(fresh(n, 0, rows), place(n, me_s, 0, rows), own_sem.at[n]),
        )

    gain_send = lambda i, shard, src, to: pltpu.make_async_remote_copy(
        src_ref=src, dst_ref=gain_out.at[shard], send_sem=gs_sem.at[i], recv_sem=gr_sem.at[i],
        device_id=to, device_id_type=MESH)
    gains = [
        gain_send(0, me_s, gain_in, to_x),
        gain_send(1, me_s, gain_in, to_core),
        gain_send(2, other, gain_out.at[other], to_core),
    ]
    gain_keep = pltpu.make_async_copy(gain_in, gain_out.at[me_s], go_sem)
    gain_keep.start()
    gains[0].start()
    gains[1].start()
    todo = [copies(n) for n in range(len(items))]
    for c in todo:
        for k in ("x", "xd", "own", "keep"):
            c[k].start()
    gains[0].wait_recv()
    gains[2].start()

    def near(c):
        c["x"].wait_recv()
        for k in ("y", "z", "c0"):
            c[k].start()

    def far(c):
        c["y"].wait_recv()
        c["fz"].start()
        c["c1"].start()
        c["z"].wait_recv()
        c["fy"].start()
        c["c2"].start()

    def end(c):
        for k in ("xd", "fy", "fz"):
            c[k].wait_recv()
        c["c3"].start()

    count = len(todo)
    for t in range(count + 2):
        if t < count:
            near(todo[t])
        if 0 <= t - 1 < count:
            far(todo[t - 1])
        if 0 <= t - 2 < count:
            end(todo[t - 2])
    for c in todo:
        for k in ("own", "c0", "c1", "c2", "c3"):
            c[k].wait_recv()
        for k in ("x", "xd", "own", "y", "z", "c0", "fz", "c1", "fy", "c2", "c3"):
            c[k].wait_send()
        c["keep"].wait()
    gains[1].wait_recv()
    gains[2].wait_recv()
    for g in gains:
        g.wait_send()
    gain_keep.wait()


def gather_all(groups, gains, n_rep, n_shard):
    tile = 16
    fits = n_shard == 4 and n_rep >= 4 and all(w.shape[0] % (4 * tile) == 0 for g in groups for w in g)
    if not fits:
        full = [lax.all_gather(jnp.concatenate(g, axis=1), "shard", axis=0, tiled=True) for g in groups]
        return full, lax.all_gather(gains, "shard", axis=0)
    items, ins = [], []
    for o, group in enumerate(groups):
        dst = 0
        for w in group:
            rows, cols = w.shape
            big = w.size > 2 * 256 * 1024
            row_cut = 3 if big and rows > cols and rows % (12 * tile) == 0 else 1
            col_cut = 3 if big and row_cut == 1 and cols % 384 == 0 else 1
            step, width = rows // row_cut, cols // col_cut
            for a in range(row_cut):
                for b in range(col_cut):
                    units = step // 4 // tile
                    third = units // 3
                    rest = units - 3 * third
                    turn = len(items) % 2
                    parts = [third, third + (rest > turn), third + (rest > 1 - turn)]
                    parts[0] = units - parts[1] - parts[2]
                    items.append({
                        "in": len(ins), "out": o, "row": a * step, "rows": step, "src": b * width,
                        "dst": dst + b * width, "cols": width, "parts": tuple(p * tile for p in parts)})
            ins.append(w)
            dst += cols
    outs = [
        jax.ShapeDtypeStruct((n_shard, g[0].shape[0], sum(w.shape[1] for w in g)), g[0].dtype) for g in groups]
    outs.append(jax.ShapeDtypeStruct((n_shard,) + gains.shape, gains.dtype))
    n = len(items)
    dma = pltpu.SemaphoreType.DMA
    hbm = pl.BlockSpec(memory_space=pltpu.HBM)
    got = pl.pallas_call(
        functools.partial(gather_kernel, {"items": items, "n_in": len(ins) + 1, "n_out": len(outs)}),
        name="gather_weights",
        out_shape=tuple(outs),
        in_specs=[hbm] * (len(ins) + 1),
        out_specs=[hbm] * len(outs),
        scratch_shapes=[dma((n, 11)), dma((n, 11)), dma((n,)), dma((3,)), dma((3,)), dma],
        compiler_params=pltpu.CompilerParams(collective_id=1, has_side_effects=True),
    )(*ins, gains)
    return [g.reshape(-1, g.shape[-1]) for g in got[:-1]], got[-1]


def sum_kernel(cfg, lt_ref, r_ref, g_ref, *refs):
    n_sets = len(cfg["sets"])
    out_refs, gout_ref, scratch = refs[:n_sets], refs[n_sets], refs[n_sets + 1 :]
    n_rep, n_shard, tok = cfg["n_rep"], cfg["n_shard"], cfg["tok"]
    sub, cols, pr, pc = cfg["sub"], cfg["cols"], cfg["pr"], cfg["pc"]
    depth, n_down, n_mid, n_qkv, n_all = (cfg[k] for k in ("depth", "n_down", "n_mid", "n_qkv", "n_all"))
    lsegs, rsegs = cfg["lsegs"], cfg["rsegs"]
    s_bits, r_bits = bit_count(n_shard), bit_count(n_rep)
    n_half = n_shard // 2
    steps = [("shard", i) for i in reversed(range(1, s_bits))] + [("rep", i) for i in range(r_bits)]
    back = [("rep", i) for i in reversed(range(r_bits))]
    n_down_steps, n_back = len(steps), len(back)
    ltf, rf, dsend = scratch[:3]
    recv = scratch[3 : 3 + n_down_steps]
    outb, gacc, grecv = scratch[3 + n_down_steps : 6 + n_down_steps]
    (ex_send, ex_recv, ex_own, send_sem, recv_sem, out_sem, g_send, g_recv, g_out) = scratch[6 + n_down_steps :]
    slots = dsend.shape[0]

    me_s, me_r = lax.axis_index("shard"), lax.axis_index("rep")
    core = me_s & 1

    def bit_of(axis, bit):
        return ((me_s if axis == "shard" else me_r) >> bit) & 1

    def peer(axis, bit):
        return {axis: (me_s if axis == "shard" else me_r) ^ (1 << bit)}

    everyone = [("shard", i) for i in range(s_bits)] + [("rep", i) for i in range(r_bits)]
    barrier = pltpu.get_barrier_semaphore()
    for axis, bit in everyone:
        pl.semaphore_signal(barrier, inc=1, device_id=peer(axis, bit), device_id_type=MESH)
    pl.semaphore_wait(barrier, len(everyone))

    def exchange(i):
        (l0, l1), (r0, r1) = lsegs[i], rsegs[i]
        remote = [
            pltpu.make_async_remote_copy(
                src_ref=lt_ref.at[1 - core, :, pl.ds(l0, l1 - l0)],
                dst_ref=ltf.at[:, pl.ds(l0, l1 - l0), pl.ds(tok, tok)],
                send_sem=ex_send.at[i, 0], recv_sem=ex_recv.at[i, 0],
                device_id=peer("shard", 0), device_id_type=MESH),
            pltpu.make_async_remote_copy(
                src_ref=r_ref.at[:, pl.ds(r0, r1 - r0)],
                dst_ref=rf.at[pl.ds(tok, tok), pl.ds(r0, r1 - r0)],
                send_sem=ex_send.at[i, 1], recv_sem=ex_recv.at[i, 1],
                device_id=peer("shard", 0), device_id_type=MESH),
        ]
        local = [
            pltpu.make_async_copy(
                lt_ref.at[core, :, pl.ds(l0, l1 - l0)],
                ltf.at[:, pl.ds(l0, l1 - l0), pl.ds(0, tok)], ex_own.at[i, 0]),
            pltpu.make_async_copy(
                r_ref.at[:, pl.ds(r0, r1 - r0)], rf.at[pl.ds(0, tok), pl.ds(r0, r1 - r0)], ex_own.at[i, 1]),
        ]
        return remote + local

    for i in range(3):
        for cp in exchange(i):
            cp.start()

    gacc[0] = g_ref[...]

    def gain_copy(i):
        axis, bit = everyone[i]
        return pltpu.make_async_remote_copy(
            src_ref=gacc.at[i], dst_ref=grecv.at[i], send_sem=g_send.at[i], recv_sem=g_recv.at[i],
            device_id=peer(axis, bit), device_id_type=MESH)

    def place(k, j):
        kk = k - n_down
        down = k < n_down
        off = jnp.where(kk < n_mid, lsegs[1][0], jnp.where(kk < n_mid + n_qkv, lsegs[2][0], cfg["lout"]))
        lrow = jnp.where(down, k * sub, off + j * sub)
        rcol = jnp.where(down, j * cols, depth + kk * cols)
        return pl.multiple_of(lrow, sub), pl.multiple_of(rcol, cols)

    def product(blk, k, j):
        lrow, rcol = place(k, j)
        return jnp.dot(
            ltf[blk, pl.ds(lrow, sub), :], rf[:, pl.ds(rcol, cols)], preferred_element_type=jnp.float32)

    rows_p, cols_p = sub // pr, cols // pc

    def pieces(j):
        for a in range(rows_p):
            for b in range(cols_p):
                yield (j * rows_p + a) * cols_p + b, a * pr, b * pc

    nb = n_half // 2
    top = bit_of(*steps[0])

    def rs_copy(i, k):
        axis, bit = steps[i]
        if i == 0:
            src = dsend.at[k % slots]
        else:
            half = recv[i - 1].shape[1] // 2
            src = recv[i - 1].at[k, pl.ds((1 - bit_of(axis, bit)) * half, half)]
        return pltpu.make_async_remote_copy(
            src_ref=src, dst_ref=recv[i].at[k], send_sem=send_sem.at[i, k], recv_sem=recv_sem.at[i, k],
            device_id=peer(axis, bit), device_id_type=MESH)

    def own_start(size):
        at = 0
        for n, (axis, bit) in enumerate(steps[s_bits - 1 :]):
            block = n_rep >> (n + 1)
            if block >= size:
                at = at + bit_of(axis, bit) * block
        return at

    def ag_copy(i, k):
        axis, bit = back[i]
        size = 1 << i
        at = pl.ds(own_start(size), size)
        n = n_down_steps + i
        return pltpu.make_async_remote_copy(
            src_ref=outb.at[k, at], dst_ref=outb.at[k, at], send_sem=send_sem.at[n, k], recv_sem=recv_sem.at[n, k],
            device_id=peer(axis, bit), device_id_type=MESH)

    def out_copies(n, k):
        lo = cfg["sets"][n][0]
        made = []
        for j in range(2):
            for b in range(cols_p):
                if n == 0:
                    dst = out_refs[n].at[k, :, :, pl.ds(j * cols + b * pc, pc)]
                else:
                    at = pl.multiple_of((k - lo) * cols, cols) + b * pc
                    dst = out_refs[n].at[pl.ds(j * rows_p, rows_p), :, pl.ds(at, pc)]
                if cols_p == 1:
                    made.append((outb.at[k, pl.ds(j * rows_p, rows_p)], dst))
                else:
                    made += [
                        (outb.at[k, (j * rows_p + a) * cols_p + b], dst.at[a]) for a in range(rows_p)]
        return [pltpu.make_async_copy(src, dst, out_sem.at[k, i]) for i, (src, dst) in enumerate(made)]

    def each_set(k, act):
        for n, (lo, hi) in enumerate(cfg["sets"]):
            @pl.when((k >= lo) & (k < hi))
            def _(n=n):
                for cp in out_copies(n, k):
                    act(cp)

    def first(k):
        for i in range(nb):
            for j in range(2):
                part = product((1 - top) * nb + i, k, j).astype(jnp.bfloat16)
                for p, a, b in pieces(j):
                    dsend[k % slots, i * n_rep + p] = part[a : a + pr, b : b + pc]

    def join(i, k):
        rs_copy(i, k).wait()
        if i == 0:
            for n in range(nb):
                for j in range(2):
                    part = product(top * nb + n, k, j)
                    for p, a, b in pieces(j):
                        q = n * n_rep + p
                        got = recv[0][k, q].astype(jnp.float32)
                        recv[0][k, q] = (part[a : a + pr, b : b + pc] + got).astype(jnp.bfloat16)
            return
        half = recv[i].shape[1]
        base = bit_of(*steps[i]) * half
        for q in range(half):
            kept = recv[i - 1][k, base + q].astype(jnp.float32)
            both = (kept + recv[i][k, q].astype(jnp.float32)).astype(jnp.bfloat16)
            if i == n_down_steps - 1:
                outb[k, own_start(1)] = both
            else:
                recv[i][k, q] = both

    lag = [0, 2]
    for _ in range(n_down_steps - 1 + n_back):
        lag.append(lag[-1] + 2)
    last = lag[-1]

    def during(t, n, do):
        k = t - lag[n]

        @pl.when((k >= 0) & (k < n_all))
        def _():
            do(k)

    def body(t, carry):
        for i, when in ((0, 0), (1, n_down), (2, n_down + n_mid)):
            @pl.when(t == when)
            def _(i=i):
                for n, cp in enumerate(exchange(i)):
                    cp.wait()

        during(t, 0, first)
        for i in range(n_down_steps):
            during(t, 1 + i, functools.partial(join, i))
        for i in range(n_back):
            during(t, 1 + n_down_steps + i, lambda k, i=i: ag_copy(i, k).wait())
        for g in range(len(everyone)):
            @pl.when(t == 3 + 2 * g)
            def _(g=g):
                gain_copy(g).wait()
                gacc[g + 1] = gacc[g] + grecv[g]

        for i in range(n_down_steps):
            during(t, i, lambda k, i=i: rs_copy(i, k).start())
        for i in range(n_back):
            during(t, n_down_steps + i, lambda k, i=i: ag_copy(i, k).start())
        during(t, n_down_steps + n_back, lambda k: each_set(k, lambda cp: cp.start()))
        for g in range(len(everyone)):
            @pl.when(t == 1 + 2 * g)
            def _(g=g):
                gain_copy(g).start()

        return carry

    lax.fori_loop(0, n_all + last, body, 0)
    gout = pltpu.make_async_copy(gacc.at[len(everyone)], gout_ref, g_out)
    gout.start()

    def finish(k, carry):
        each_set(k, lambda cp: cp.wait())
        return carry

    lax.fori_loop(0, n_all, finish, 0)
    gout.wait()


def reduce_grads(hid, h2, h1, ob, dyb, dgate, dup, dqkv, dx2b, gains, n_rep, n_shard):
    tok, ff = hid.shape
    depth = h1.shape[1]
    qkv = dqkv.shape[1]
    n_half = n_shard // 2
    sub = depth // n_shard // 2
    cols = depth // 2
    pr = max(16, 2 * sub // n_rep)
    pc = cols * (2 * sub // pr) // n_rep
    n_down, n_mid, n_qkv, n_out = ff // cols, 2 * ff // cols, qkv // cols, depth // cols
    n_all = n_down + n_mid + n_qkv + n_out
    fs, ds = ff // n_shard, depth // n_shard
    lt = jnp.concatenate([v.T.reshape(n_shard, -1, tok) for v in (hid, h2, h1, ob)], axis=1)
    lt = lt.reshape(n_half, 2, -1, tok).transpose(1, 0, 2, 3)
    right = jnp.concatenate([dyb, dgate, dup, dqkv, dx2b], axis=1)
    lrows, rcols = lt.shape[2], right.shape[1]
    cfg = dict(
        n_rep=n_rep, n_shard=n_shard, tok=tok, sub=sub, cols=cols, pr=pr, pc=pc, depth=depth,
        n_down=n_down, n_mid=n_mid, n_qkv=n_qkv, n_all=n_all, lout=fs + 2 * ds,
        lsegs=((0, fs), (fs, fs + ds), (fs + ds, lrows)),
        rsegs=((0, depth), (depth, depth + 2 * ff), (depth + 2 * ff, rcols)),
    )
    g_rows = gains.shape[0]
    ends = [n_down, n_down + n_mid // 2, n_down + n_mid, n_down + n_mid + n_qkv, n_all]
    cfg["sets"] = tuple(zip([0] + ends[:-1], ends))
    rp, cp = sub // pr, cols // pc
    shapes = [(n_down, rp, pr, depth)] + [(2 * rp, pr, n) for n in (ff, ff, qkv, depth)]
    s_bits, r_bits = bit_count(n_shard), bit_count(n_rep)
    n_hops = s_bits + r_bits
    n_steps = s_bits - 1 + r_bits
    slots = 4
    sizes = [n_half * n_rep >> (i + 1) for i in range(n_steps)]
    bf = jnp.bfloat16
    dma = pltpu.SemaphoreType.DMA
    *outs, gsum = pl.pallas_call(
        functools.partial(sum_kernel, cfg),
        name="sum_grads",
        out_shape=(
            *[jax.ShapeDtypeStruct(shape, bf) for shape in shapes],
            jax.ShapeDtypeStruct((g_rows, 128), jnp.float32),
        ),
        in_specs=[pl.BlockSpec(memory_space=pltpu.VMEM)] * 3,
        out_specs=[pl.BlockSpec(memory_space=pltpu.HBM)] * (len(shapes) + 1),
        scratch_shapes=[
            pltpu.VMEM((n_half, lrows, 2 * tok), bf),
            pltpu.VMEM((2 * tok, rcols), bf),
            pltpu.VMEM((slots, sizes[0], pr, pc), bf),
            *[pltpu.VMEM((n_all, size, pr, pc), bf) for size in sizes],
            pltpu.VMEM((n_all, n_rep, pr, pc), bf),
            pltpu.VMEM((n_hops + 1, g_rows, 128), jnp.float32),
            pltpu.VMEM((n_hops, g_rows, 128), jnp.float32),
            dma((3, 2)), dma((3, 2)), dma((3, 2)),
            dma((n_steps + r_bits, n_all)), dma((n_steps + r_bits, n_all)), dma((n_all, 2 if cp == 1 else n_rep)),
            dma((n_hops,)), dma((n_hops,)), dma,
        ],
        compiler_params=pltpu.CompilerParams(
            collective_id=0, has_side_effects=True, vmem_limit_bytes=60_000_000),
    )(lt, right, gains)

    return [v.reshape(-1, v.shape[-1]).astype(jnp.float32) for v in outs], gsum


def local(
    n_rep,
    n_shard,
    tokens,
    cotangent,
    doc_ids,
    w_query,
    w_key,
    w_value,
    w_out,
    w_gate,
    w_up,
    w_down,
    gain_attn,
    gain_ffn,
    gain_query,
    gain_key,
):
    tok_rows, width = tokens.shape
    ff = w_gate.shape[1]
    q_width, k_width = w_query.shape[1], w_key.shape[1]
    head_share = QH // KVH
    score_scale = 1.0 / math.sqrt(HEAD_DIM)
    gains = (gain_attn, gain_ffn, gain_query, gain_key)
    gain_sizes = [g.shape[0] for g in gains]
    gain_ends = [sum(gain_sizes[: i + 1]) for i in range(len(gains))]
    flat_gains = jnp.concatenate(gains)
    n_gain = flat_gains.shape[0]
    flat_gains = jnp.pad(flat_gains, (0, -n_gain % 2048)).reshape(-1, 128)
    (qkv_set, out_set, gate_set, up_set, down_set), all_gains = gather_all(
        [[w_query, w_key, w_value], [w_out], [w_gate], [w_up], [w_down]], flat_gains, n_rep, n_shard
    )
    all_gains = all_gains.reshape(n_shard, -1)
    full_gattn, full_gffn, full_gquery, full_gkey = (
        all_gains[:, end - size : end].reshape(-1) for size, end in zip(gain_sizes, gain_ends)
    )

    doc_rows = doc_ids[None, :]
    allowed, positions = doc_tables(doc_rows)
    key_mask = allowed[:, None, None]
    cos_tab, sin_tab = rope_tables(positions, HEAD_DIM)
    resid_in = tokens.astype(jnp.float32)
    normed_in, unit_in, rms_in = norm_rows(resid_in, full_gattn)
    normed_bf = normed_in.astype(jnp.bfloat16)
    qkv = matmul(normed_bf, qkv_set)
    query_raw = qkv[:, :q_width].reshape(1, tok_rows, QH, HEAD_DIM)
    key_raw = qkv[:, q_width : q_width + k_width].reshape(1, tok_rows, KVH, HEAD_DIM)
    value_bf = qkv[:, q_width + k_width :].astype(jnp.bfloat16).reshape(1, tok_rows, KVH, HEAD_DIM)
    query_normed, query_unit, query_rms = norm_rows(query_raw, full_gquery)
    key_normed, key_unit, key_rms = norm_rows(key_raw, full_gkey)
    query_bf = (
        rotate(query_normed, cos_tab, sin_tab)
        .astype(jnp.bfloat16)
        .reshape(1, tok_rows, KVH, head_share, HEAD_DIM)
    )
    key_bf = rotate(key_normed, cos_tab, sin_tab).astype(jnp.bfloat16)
    attn_probs, log_total = attn_probs_of(query_bf, key_bf, key_mask, None, score_scale)
    probs_bf = attn_probs.astype(jnp.bfloat16)
    mixed_bf = (
        jnp.einsum("gkrqs,gskd->gqkrd", probs_bf, value_bf, preferred_element_type=jnp.float32)
        .astype(jnp.bfloat16)
        .reshape(tok_rows, QH * HEAD_DIM)
    )
    resid_mid = resid_in + matmul(mixed_bf, out_set)
    normed_mid, unit_mid, rms_mid = norm_rows(resid_mid, full_gffn)
    hidden_in = normed_mid.astype(jnp.bfloat16)
    gate_proj = matmul(hidden_in, gate_set)
    up_proj = matmul(hidden_in, up_set)
    gate_sig = jax.nn.sigmoid(gate_proj)
    gate_act = gate_proj * gate_sig
    hidden_bf = (gate_act * up_proj).astype(jnp.bfloat16)

    live_rows = (doc_ids >= 0).astype(jnp.float32)[:, None]
    grad_y = cotangent.astype(jnp.float32) * live_rows
    grad_y_bf = grad_y.astype(jnp.bfloat16)
    block_out = (resid_mid + matmul(hidden_bf, down_set)).astype(jnp.bfloat16)

    grad_hidden = matmul_t(grad_y_bf, down_set)
    grad_gate_bf = (grad_hidden * up_proj * gate_sig * (1.0 + gate_proj * (1.0 - gate_sig))).astype(
        jnp.bfloat16
    )
    grad_up_bf = (grad_hidden * gate_act).astype(jnp.bfloat16)
    grad_norm_mid = matmul_t(grad_gate_bf, gate_set) + matmul_t(grad_up_bf, up_set)
    back_mid, part_gffn = norm_back(grad_norm_mid, unit_mid, rms_mid, full_gffn)
    grad_mid = grad_y + back_mid
    grad_mid_bf = grad_mid.astype(jnp.bfloat16)
    grad_mixed_bf = (
        matmul_t(grad_mid_bf, out_set)
        .astype(jnp.bfloat16)
        .reshape(1, tok_rows, KVH, head_share, HEAD_DIM)
    )
    grad_scores = jnp.einsum(
        "gqkrd,gskd->gkrqs", grad_mixed_bf, value_bf, preferred_element_type=jnp.float32
    )
    grad_value_bf = (
        jnp.einsum("gkrqs,gqkrd->gskd", probs_bf, grad_mixed_bf, preferred_element_type=jnp.float32)
        .astype(jnp.bfloat16)
        .reshape(tok_rows, KVH * HEAD_DIM)
    )
    row_dot = jnp.sum(attn_probs * grad_scores, axis=-1, keepdims=True)
    grad_logits = (attn_probs * (grad_scores - row_dot) * score_scale).astype(jnp.bfloat16)
    grad_query_rot = jnp.einsum(
        "gkrqs,gskd->gqkrd", grad_logits, key_bf, preferred_element_type=jnp.float32
    ).reshape(1, tok_rows, QH, HEAD_DIM)
    grad_key_rot = jnp.einsum(
        "gkrqs,gqkrd->gskd", grad_logits, query_bf, preferred_element_type=jnp.float32
    )
    grad_query_raw, part_gquery = norm_back(
        rotate_back(grad_query_rot, cos_tab, sin_tab), query_unit, query_rms, full_gquery
    )
    grad_key_raw, part_gkey = norm_back(
        rotate_back(grad_key_rot, cos_tab, sin_tab), key_unit, key_rms, full_gkey
    )
    grad_query_bf = grad_query_raw.astype(jnp.bfloat16).reshape(tok_rows, QH * HEAD_DIM)
    grad_key_bf = grad_key_raw.astype(jnp.bfloat16).reshape(tok_rows, KVH * HEAD_DIM)
    grad_qkv_bf = jnp.concatenate([grad_query_bf, grad_key_bf, grad_value_bf], axis=1)
    grad_norm_in = matmul_t(grad_qkv_bf, qkv_set)
    back_in, part_gattn = norm_back(grad_norm_in, unit_in, rms_in, full_gattn)
    grad_tokens = grad_mid + back_in
    part_gains = jnp.concatenate(
        [
            p.reshape(n_shard, -1)
            for p in (part_gattn, part_gffn, part_gquery, part_gkey)
        ],
        axis=1,
    )
    part_gains = part_gains.astype(jnp.bfloat16).astype(jnp.float32)
    flat = part_gains.reshape(-1)
    flat = jnp.pad(flat, (0, -flat.shape[0] % 1024)).reshape(-1, 128)
    (grad_down, grad_gate, grad_up, grad_qkv, grad_out), sum_gains = reduce_grads(
        hidden_bf, hidden_in, normed_bf, mixed_bf,
        grad_y_bf, grad_gate_bf, grad_up_bf, grad_qkv_bf, grad_mid_bf,
        flat, n_rep, n_shard,
    )
    ends = [q_width, q_width + k_width]
    grad_query, grad_key, grad_value = jnp.split(grad_qkv, ends, axis=1)
    sum_gains = sum_gains.reshape(-1)[: part_gains.size].reshape(part_gains.shape)
    own_gains = lax.dynamic_index_in_dim(sum_gains, lax.axis_index("shard"), axis=0, keepdims=False)
    grad_gattn, grad_gffn, grad_gquery, grad_gkey = (
        own_gains[end - size : end] for size, end in zip(gain_sizes, gain_ends)
    )
    return (
        block_out,
        grad_tokens,
        grad_query,
        grad_key,
        grad_value,
        grad_out,
        grad_gate,
        grad_up,
        grad_down,
        grad_gattn,
        grad_gffn,
        grad_gquery,
        grad_gkey,
    )


def solution(mesh):
    return jax.shard_map(
        functools.partial(local, mesh.shape["rep"], mesh.shape["shard"]),
        mesh=mesh,
        in_specs=(
            P(("rep", "shard"), None),
            P(("rep", "shard"), None),
            P(("rep", "shard")),
            P("shard", None),
            P("shard", None),
            P("shard", None),
            P("shard", None),
            P("shard", None),
            P("shard", None),
            P("shard", None),
            P("shard"),
            P("shard"),
            P("shard"),
            P("shard"),
        ),
        out_specs=(
            P(("rep", "shard"), None),
            P(("rep", "shard"), None),
            P("shard", None),
            P("shard", None),
            P("shard", None),
            P("shard", None),
            P("shard", None),
            P("shard", None),
            P("shard", None),
            P("shard"),
            P("shard"),
            P("shard"),
            P("shard"),
        ),
        check_vma=False,
    )
```

profile of v0, /device:TPU:0, one launch (start us, length us, event | category | flops | bytes accessed | tf_op | source)
XLA Modules:
  0.0 618.3 jit_solution(11334613553564867877)
XLA Ops:
  0.6 1.4 fusion.51.refs_7_
  2.0 269.1 %gather_weights.1 = (bf16[4,256,2048]{2,1,0:T(8,128)(2,1)}, bf16[4,256,1024]{2,1,0:T(8,128)(2,1)}, bf16[4,256,4608]{2,1,0:T(8,128)(2,1)}, bf16[4,256,4608]{2,1,0...) custom-call(bf16[256,1024]{1,0:T(8,128)(2,1)} %refs_0_.1, bf16[256,512]{1,0:T(8,128)(2,1)} %refs_1_.1, ...), custom_call_target="tpu_custom_call" | custom-call | tf_op jit(solution)/shard_map/gather_weights/pallas_call | solution.py:245
  271.1 0.7 copy.114
  272.0 3.0 fusion.36
  279.0 5.3 fusion.61
  284.3 0.8 fusion.31
  285.3 4.7 fusion.32
  290.0 5.5 constant_dynamic-update-slice_fusion.4
  295.5 6.9 %fusion.6 = bf16[128,1024]{1,0:T(8,128)(2,1)} fusion(f32[128,1024]{1,0:T(8,128)S(1)} %get-tuple-element.77, bf16[4608,1024]{1,0:T(8,128)(2,1)} %bitcast.175, f32[128,4608]{1,0:T(8,128)S(1)} %fusion.61, f32[128,4608]{1,0:T(8,128)S(1)} %get-tuple-element.78), kind=kOutput, calls=%fused_computation.22 | convolution fusion | flops 1211760640 | bytes 14942208 | tf_op jit(solution)/shard_map/dot_general | solution.py:23
  302.4 4.7 fusion.62
  307.1 3.3 constant_dynamic-update-slice_fusion.3
  310.5 3.7 multiply_reduce_fusion.2
  314.4 1.5 convolution_convert_fusion
  315.9 1.8 copy.77
  317.7 1.9 fusion.7
  319.7 1.7 copy.89
  321.3 1.5 mul.572
  322.8 2.0 copy.82
  324.9 1.4 multiply_reduce_fusion
  327.4 0.9 pad_maximum_fusion
  328.4 1.0 copy.81
  329.4 1.2 copy.79
  330.7 2.1 constant_dynamic-update-slice_fusion.2
  332.8 0.7 mul.592
  333.6 1.8 copy.87
  335.4 1.5 convolution_bitcast_fusion.2
  336.8 0.8 multiply_add_fusion.2
  337.6 1.7 pad_maximum_fusion.2
  339.5 1.1 copy.84
  340.6 0.7 mul.598
  341.3 1.7 constant_dynamic-update-slice_fusion.1
  343.1 3.8 fusion.22
  346.9 0.9 fusion.19
  347.8 1.0 fusion.18
  348.9 1.1 concatenate.97
  350.0 0.9 copy.93
  351.2 0.9 copy.92
  352.1 4.0 fusion
  356.2 2.4 copy.90
  358.6 2.9 maximum_bitcast_fusion.lt_ref
  362.2 0.7 convert_dynamic-update-slice_fusion.r_ref
  364.3 239.5 %sum_grads.1 = (bf16[9,4,32,1024]{3,2,1,0:T(8,128)(2,1)}, bf16[8,32,4608]{2,1,0:T(8,128)(2,1)}, bf16[8,32,4608]{2,1,0:T(8,128)(2,1)}, bf16[8,32,2048]{2,1,0:T(8,...) custom-call(bf16[2,2,1920,128]{3,2,1,0:T(8,128)(2,1)} %maximum_bitcast_fusion.lt_ref, ...), custom_call_target="tpu_custom_call" | custom-call | tf_op jit(solution)/shard_map/sum_grads/pallas_call | solution.py:516
  603.8 1.5 bitcast_convert_fusion.3
  605.3 1.0 split.12
  606.3 1.0 fusion.59
  607.4 1.1 bitcast_convert_fusion.4
  608.8 5.3 bitcast_convert_fusion.1
  614.1 2.9 bitcast_convert_fusion
  (190 shorter events, 9.5 us)
Async XLA Ops:
  2.0 269.8 %copy-start.8 = (bf16[128,1024]{1,0:T(8,128)(2,1)S(1)}, bf16[128,1024]{1,0:T(8,128)(2,1)}, u32[]{:S(2)}) copy-start(bf16[128,1024]{1,0:T(8,128)(2,1)} %param.14) | copy-start | bytes 786436
  271.8 3.2 copy-start.41
  272.0 3.0 copy-start.52
  272.0 3.2 copy-start.54
  275.3 2.7 copy-start.29
  275.7 1.7 copy-start.6
  276.2 1.6 copy-start.27
  276.3 1.6 copy-start.25
  276.4 1.8 copy-start.51
  276.6 1.7 copy-start.4
  277.9 6.3 %copy-start.37 = (f32[8,2,128]{2,1,0:T(2,128)}, f32[8,2,128]{2,1,0:T(2,128)S(1)}, u32[]{:S(2)}) copy-start(f32[8,2,128]{2,1,0:T(2,128)S(1)} %log.8) | copy-start | bytes 24580
  278.3 6.0 copy-start.21
  278.3 6.0 copy-start.20
  278.9 35.3 %copy-start.31 = (f32[1,2,4,128]{3,1,2,0:T(2,128)}, f32[1,2,4,128]{3,1,2,0:T(2,128)S(1)}, u32[]{:S(2)}) copy-start(f32[1,2,4,128]{3,1,2,0:T(2,128)S(1)} %copy.108) | copy-start | bytes 12292
  278.9 35.3 %copy-start.45 = (f32[128]{0:T(128)}, f32[128]{0:T(128)S(1)}, u32[]{:S(2)}) copy-start(f32[128]{0:T(128)S(1)} %add_rsqrt_fusion.2) | copy-start | bytes 1540
  278.9 6.4 %copy-start.1 = (bf16[4,1152,1024]{2,1,0:T(8,128)(2,1)S(1)}, bf16[4,1152,1024]{2,1,0:T(8,128)(2,1)}, u32[]{:S(2)}) copy-start(bf16[4,1152,1024]{2,1,0:T(8,128)(2,1)} %get-tuple-element.30) | copy-start | bytes 28311556
  278.9 11.0 %slice-start.3 = ((s8[9437184]{0:T(1024)(128)(4,1)}), s8[4194304]{0:T(1024)(128)(4,1)S(1)}, s32[]{:S(2)}) async-start(s8[9437184]{0:T(1024)(128)(4,1)} %bitcast.171), calls=%async_computation.3 | async-start | bytes 8388608
  278.9 11.0 %slice-start.4 = ((s8[9437184]{0:T(1024)(128)(4,1)}), s8[4194304]{0:T(1024)(128)(4,1)S(1)}, s32[]{:S(2)}) async-start(s8[9437184]{0:T(1024)(128)(4,1)} %bitcast.171), calls=%async_computation.4 | async-start | bytes 8388608
  284.3 11.2 %copy-start = (f32[128,4608]{1,0:T(8,128)}, f32[128,4608]{1,0:T(8,128)S(1)}, u32[]{:S(2)}) copy-start(f32[128,4608]{1,0:T(8,128)S(1)} %fusion.61) | copy-start | bytes 7077892
  285.3 4.7 slice-start.5
  290.0 20.4 %slice-start = ((s8[9437184]{0:T(1024)(128)(4,1)}), s8[4194304]{0:T(1024)(128)(4,1)S(1)}, s32[]{:S(2)}) async-start(s8[9437184]{0:T(1024)(128)(4,1)} %bitcast.166), calls=%async_computation | async-start | bytes 8388608
  295.5 6.9 %copy-start.2 = (f32[128,4608]{1,0:T(8,128)}, f32[128,4608]{1,0:T(8,128)S(1)}, u32[]{:S(2)}) copy-start(f32[128,4608]{1,0:T(8,128)S(1)} %get-tuple-element.78) | copy-start | bytes 7077892
  295.5 15.0 %slice-start.1 = ((s8[9437184]{0:T(1024)(128)(4,1)}), s8[4194304]{0:T(1024)(128)(4,1)S(1)}, s32[]{:S(2)}) async-start(s8[9437184]{0:T(1024)(128)(4,1)} %bitcast.166), calls=%async_computation.1 | async-start | bytes 8388608
  295.5 15.0 %slice-start.2 = ((s8[9437184]{0:T(1024)(128)(4,1)}), s8[1048576]{0:T(1024)(128)(4,1)S(1)}, s32[]{:S(2)}) async-start(s8[9437184]{0:T(1024)(128)(4,1)} %bitcast.166), calls=%async_computation.2 | async-start | bytes 2097152
  302.4 4.7 copy-start.3
  310.4 3.9 copy-start.5
  324.9 1.8 copy-start.34
  324.9 1.8 copy-start.36
  326.7 1.6 copy-start.12
  327.1 3.6 copy-start.9
  328.4 4.5 copy-start.44
  330.6 7.0 %copy-start.10 = (f32[128,1024]{1,0:T(8,128)}, f32[128,1024]{1,0:T(8,128)S(1)}, u32[]{:S(2)}) copy-start(f32[128,1024]{1,0:T(8,128)S(1)} %copy.79) | copy-start | bytes 1572868
  335.3 7.7 %copy-start.23 = (bf16[128,512]{1,0:T(8,128)(2,1)S(1)}, bf16[128,512]{1,0:T(8,128)(2,1)}, u32[]{:S(2)}) copy-start(bf16[128,512]{1,0:T(8,128)(2,1)} %copy.89) | copy-start | bytes 393220
  340.6 2.5 copy-start.18
  343.0 3.8 copy-start.42
  343.0 3.8 copy-start.53
  346.9 4.0 copy-start.32
  346.9 4.0 copy-start.46
  356.2 2.4 copy-start.22
  358.6 4.3 copy-start.17
  358.6 4.3 copy-start.19
  358.6 4.6 copy-start.11
  361.5 2.0 copy-start.50
  605.3 2.1 copy-start.24
  605.3 3.2 copy-start.16
  606.3 2.5 copy-start.15
  608.8 5.3 copy-start.14
  614.1 2.9 copy-start.47
  (13 other events, 14.6 us)
where the time goes:
time: 619 us; the launch traced here: 618 us
  Pallas kernels  509 us (82%)
  matrix products  45.4 us (7%)
  other arithmetic  35.7 us (6%)
  local copies, waits for them, and re-layouts  27 us (4%)
    pallas_call x1, Pallas kernels, gather_all(): pl.pallas_call(functools.partial(gather_kernel, {'items': items, 'n_in':...  269 us
    pallas_call x1, Pallas kernels, reduce_grads(): pl.pallas_call(functools.partial(sum_kernel, cfg), name='sum_grads', out_...  239 us
    dot_general x5, matrix products, matmul(): return jnp.dot(left, right, preferred_element_type=jnp.float32)  21.2 us
    dot_general x5, matrix products, matmul_t(): lax.dot_general(left, right, (((1,), (1,)), ((), ())), preferred_element_...  18.4 us

commit v1 on v0

--- a/solution.py
+++ b/solution.py
@@ -98,7 +98,8 @@
     items, n_in, n_out = cfg["items"], cfg["n_in"], cfg["n_out"]
     ins, outs = refs[:n_in], refs[n_in : n_in + n_out]
     gain_in, gain_out = ins[-1], outs[-1]
-    send_sem, recv_sem, own_sem, gs_sem, gr_sem, go_sem = refs[n_in + n_out :]
+    held = refs[n_in + n_out : n_in + 2 * n_out - 1]
+    send_sem, recv_sem, own_sem, out_sem, gs_sem, gr_sem, go_sem = refs[n_in + 2 * n_out - 1 :]
     me_s, me_r = lax.axis_index("shard"), lax.axis_index("rep")
     core, y, z = me_s & 1, me_r & 1, (me_r >> 1) & 1
     peers = [{"shard": me_s ^ 1}, {"shard": me_s ^ 2}, {"rep": me_r ^ 1}, {"rep": me_r ^ 2}]
@@ -114,6 +115,10 @@
 
     def place(n, shard, row, size):
         it = items[n]
+        return held[it["out"]].at[shard, pl.ds(it["row"] + row, size), pl.ds(it["dst"], it["cols"])]
+
+    def result(n, shard, row, size):
+        it = items[n]
         return outs[it["out"]].at[shard, pl.ds(it["row"] + row, size), pl.ds(it["dst"], it["cols"])]
 
     def fresh(n, row, size):
@@ -134,7 +139,8 @@
         rows, quarter = it["rows"], it["rows"] // 4
         dx, dy, dz = it["parts"]
         at = lambda q: pl.multiple_of(q * quarter, quarter)
-        whole = lambda i, row, size, to: send(n, i, fresh(n, row, size), place(n, me_s, row, size), to)
+        whole = lambda i, row, size, to: send(
+            n, i, place(n, me_s, row, size), place(n, me_s, row, size), to)
         return dict(
             x=whole(0, at(mine), quarter, to_x),
             xd=whole(1, at(diag), dx, to_x),
@@ -147,6 +153,10 @@
             fy=relay(n, 8, at(from_z) + dx, dy, to_y),
             c2=relay(n, 9, at(from_z), quarter, to_core),
             c3=relay(n, 10, at(diag), quarter, to_core),
+            out=[
+                pltpu.make_async_copy(
+                    place(n, me_s ^ d, 0, rows), result(n, me_s ^ d, 0, rows), out_sem.at[n, d])
+                for d in range(4)],
             keep=pltpu.make_async_copy(fresh(n, 0, rows), place(n, me_s, 0, rows), own_sem.at[n]),
         )
 
@@ -164,8 +174,12 @@
     gains[1].start()
     todo = [copies(n) for n in range(len(items))]
     for c in todo:
-        for k in ("x", "xd", "own", "keep"):
+        c["keep"].start()
+    for c in todo:
+        c["keep"].wait()
+        for k in ("x", "xd", "own"):
             c[k].start()
+        c["out"][0].start()
     gains[0].wait_recv()
     gains[2].start()
 
@@ -186,21 +200,30 @@
         for k in ("xd", "fy", "fz"):
             c[k].wait_recv()
         c["c3"].start()
+        c["out"][2].start()
+        c["own"].wait_recv()
+        c["out"][1].start()
+
+    def pair(c):
+        for k in ("c0", "c1", "c2", "c3"):
+            c[k].wait_recv()
+        c["out"][3].start()
 
     count = len(todo)
-    for t in range(count + 2):
+    for t in range(count + 3):
         if t < count:
             near(todo[t])
         if 0 <= t - 1 < count:
             far(todo[t - 1])
         if 0 <= t - 2 < count:
             end(todo[t - 2])
+        if 0 <= t - 3 < count:
+            pair(todo[t - 3])
     for c in todo:
-        for k in ("own", "c0", "c1", "c2", "c3"):
-            c[k].wait_recv()
         for k in ("x", "xd", "own", "y", "z", "c0", "fz", "c1", "fy", "c2", "c3"):
             c[k].wait_send()
-        c["keep"].wait()
+        for cp in c["out"]:
+            cp.wait()
     gains[1].wait_recv()
     gains[2].wait_recv()
     for g in gains:
@@ -248,8 +271,12 @@
         out_shape=tuple(outs),
         in_specs=[hbm] * (len(ins) + 1),
         out_specs=[hbm] * len(outs),
-        scratch_shapes=[dma((n, 11)), dma((n, 11)), dma((n,)), dma((3,)), dma((3,)), dma],
-        compiler_params=pltpu.CompilerParams(collective_id=1, has_side_effects=True),
+        scratch_shapes=[
+            *[pltpu.VMEM(o.shape, o.dtype) for o in outs[:-1]],
+            dma((n, 11)), dma((n, 11)), dma((n,)), dma((n, 4)), dma((3,)), dma((3,)), dma,
+        ],
+        compiler_params=pltpu.CompilerParams(
+            collective_id=1, has_side_effects=True, vmem_limit_bytes=44_000_000),
     )(*ins, gains)
     return [g.reshape(-1, g.shape[-1]) for g in got[:-1]], got[-1]
 

time: 619 us -> 443 us (0.72)
  Pallas kernels: 509 us -> 321 us
  local copies, waits for them, and re-layouts: 27 us -> 35.3 us
    pallas_call x1, Pallas kernels: 269 us -> 82.2 us  [gather_all(): pl.pallas_call(functools.partial(gather_kernel, {'items': items, 'n_in':...]
    unnamed x126 -> x152, local copies, waits for them, and re-layouts: 3.13 us -> 12.1 us
where the time goes in v1:
time: 443 us; the launch traced here: 442 us
  Pallas kernels  321 us (72%)
  matrix products  45.1 us (10%)
  other arithmetic  39.3 us (9%)
  local copies, waits for them, and re-layouts  35.3 us (8%)
    pallas_call x1, Pallas kernels, reduce_grads(): pl.pallas_call(functools.partial(sum_kernel, cfg), name='sum_grads', out_...  239 us
    pallas_call x1, Pallas kernels, gather_all(): pl.pallas_call(functools.partial(gather_kernel, {'items': items, 'n_in':...  82.2 us
    dot_general x5, matrix products, matmul(): return jnp.dot(left, right, preferred_element_type=jnp.float32)  21.2 us
    dot_general x5, matrix products, matmul_t(): lax.dot_general(left, right, (((1,), (1,)), ((), ())), preferred_element_...  19.1 us
    unnamed x152, local copies, waits for them, and re-layouts  12.1 us
    convert_element_type x4, other arithmetic, reduce_grads(): v.reshape(-1, v.shape[-1]).astype(jnp.float32)  10.7 us

profile of v1, /device:TPU:0, one launch (start us, length us, event | category | flops | bytes accessed | tf_op | source)
XLA Modules:
  0.0 442.0 jit_solution(767486053694257426)
XLA Ops:
  1.4 1.7 copy-done
  3.1 1.7 copy-done.1
  4.8 1.7 copy-done.2
  6.4 1.0 copy-done.3
  7.5 1.0 copy-done.4
  8.5 0.9 copy-done.5
  9.5 0.9 copy-done.6
  10.4 82.2 %gather_weights.1 = (bf16[4,256,2048]{2,1,0:T(8,128)(2,1)}, bf16[4,256,1024]{2,1,0:T(8,128)(2,1)S(1)}, bf16[4,256,4608]{2,1,0:T(8,128)(2,1)}, bf16[4,256,4608]{2...) custom-call(bf16[256,1024]{1,0:T(8,128)(2,1)S(1)} %copy-done.3, ...), custom_call_target="tpu_custom_call" | custom-call | tf_op jit(solution)/shard_map/gather_weights/pallas_call | solution.py:268
  93.4 3.0 fusion.36
  97.1 1.0 copy.73
  98.1 1.4 fusion.40
  101.0 0.8 slice.104
  101.8 2.0 copy.75
  103.9 1.1 multiply_reduce_fusion.6
  105.0 1.2 multiply_multiply_fusion
  107.3 1.3 reshape.727
  109.3 1.1 copy.74
  112.0 1.4 select_reduce_fusion
  114.6 5.3 %fusion.61 = f32[128,4608]{1,0:T(8,128)S(1)} fusion(bf16[1024,4608]{1,0:T(8,128)(2,1)} %bitcast.168, f32[128,1024]{1,0:T(8,128)S(1)} %get-tuple-element.77, f32[1024]{0:T(1024)S(1)} %bitcast.203, f32[128]{0:T(128)S(1)} %add_rsqrt_fusion.2), kind=kOutput, calls=%fused_computation.145 | convolution fusion | flops 1208352768 | bytes 12325376 | tf_op jit(solution)/shard_map/dot_general | solution.py:23
  119.9 0.8 fusion.31
  121.3 4.7 %fusion.32 = f32[128,4608]{1,0:T(8,128)} fusion(bf16[4608,1024]{1,0:T(8,128)(2,1)S(1)} %bitcast.179, bf16[128,1024]{1,0:T(8,128)(2,1)S(1)} %copy-done.32, f32[128]{0:T(128)S(1)} %compare_convert_fusion), kind=kOutput, calls=%fused_computation.89 | convolution fusion | flops 1208352768 | bytes 12059136 | tf_op jit(solution)/shard_map/dot_general | solution.py:27
  126.0 5.4 %constant_dynamic-update-slice_fusion.4 = (bf16[128,13312]{1,0:T(8,128)(2,1)}, bf16[128,4608]{1,0:T(8,128)(2,1)}, f32[128,4608]{1,0:T(8,128)S(1)}) fusion(bf16[128,13312]{1,0:T(8,128)(2,1)} %fusion.31, f32[128,4608]{1,0:T(8,128)} %fusion.32, f32[128,4608]{1,0:T(8,128)S(1)} %fusion.61, bf16[1024,4608]{1,0:T(8,128)(2,1)S(1)} %bitcast.176, ...), kind=kOutput, calls=%fused_computation.107 | convolution fusion | flops 1214251008 | bytes 19403264 | tf_op jit(solution)/shard_map/dot_general | solution.py:23
  131.4 6.9 %fusion.6 = bf16[128,1024]{1,0:T(8,128)(2,1)} fusion(f32[128,1024]{1,0:T(8,128)S(1)} %get-tuple-element.77, bf16[4608,1024]{1,0:T(8,128)(2,1)} %bitcast.178, f32[128,4608]{1,0:T(8,128)S(1)} %fusion.61, f32[128,4608]{1,0:T(8,128)S(1)} %get-tuple-element.78), kind=kOutput, calls=%fused_computation.22 | convolution fusion | flops 1211760640 | bytes 14942208 | tf_op jit(solution)/shard_map/dot_general | solution.py:23
  138.4 5.5 %fusion.62 = f32[128,1024]{1,0:T(8,128)} fusion(bf16[128,4608]{1,0:T(8,128)(2,1)} %get-tuple-element.48, bf16[1024,4608]{1,0:T(8,128)(2,1)S(1)} %bitcast.177), kind=kOutput, calls=%fused_computation.146 | convolution fusion | flops 1207959552 | bytes 11141120 | tf_op jit(solution)/shard_map/dot_general | solution.py:27
  143.8 3.4 constant_dynamic-update-slice_fusion.3
  147.3 3.7 multiply_reduce_fusion.2
  152.0 1.5 convolution_convert_fusion
  153.5 1.1 copy.77
  154.7 1.0 fusion.7
  159.3 1.0 copy.81
  160.6 2.1 constant_dynamic-update-slice_fusion.2
  162.9 1.4 convolution_bitcast_fusion.2
  167.7 3.8 fusion.22
  171.6 0.9 fusion.19
  172.5 1.0 fusion.18
  173.5 1.1 concatenate.97
  174.7 0.9 copy.93
  175.9 0.9 copy.92
  176.8 4.0 fusion
  180.8 2.4 copy.90
  183.2 2.9 maximum_bitcast_fusion.lt_ref
  189.0 238.5 %sum_grads.1 = (bf16[9,4,32,1024]{3,2,1,0:T(8,128)(2,1)}, bf16[8,32,4608]{2,1,0:T(8,128)(2,1)}, bf16[8,32,4608]{2,1,0:T(8,128)(2,1)}, bf16[8,32,2048]{2,1,0:T(8,...) custom-call(bf16[2,2,1920,128]{3,2,1,0:T(8,128)(2,1)} %maximum_bitcast_fusion.lt_ref, ...), custom_call_target="tpu_custom_call" | custom-call | tf_op jit(solution)/shard_map/sum_grads/pallas_call | solution.py:543
  427.5 1.5 bitcast_convert_fusion.3
  429.0 1.0 split.12
  430.0 1.0 fusion.59
  431.1 1.1 bitcast_convert_fusion.4
  432.5 5.3 %bitcast_convert_fusion.1 = (f32[256,4608]{1,0:T(8,128)}, f32[256,4608]{1,0:T(8,128)}) fusion(bf16[8,32,4608]{2,1,0:T(8,128)(2,1)S(1)} %copy-done.27, bf16[8,32,4608]{2,1,0:T(8,128)(2,1)S(1)} %copy-done.26), kind=kLoop, calls=%fused_computation.1 | loop fusion | flops 2359296 | bytes 14155776 | tf_op jit(solution)/shard_map/convert_element_type | solution.py:568
  437.8 2.9 bitcast_convert_fusion
  (216 shorter events, 21.8 us)
Async XLA Ops:
  10.4 82.8 %copy-start.18 = (bf16[128,1024]{1,0:T(8,128)(2,1)S(1)}, bf16[128,1024]{1,0:T(8,128)(2,1)}, u32[]{:S(2)}) copy-start(bf16[128,1024]{1,0:T(8,128)(2,1)} %param.14) | copy-start | bytes 786436
  93.2 3.1 copy-start.53
  93.4 3.0 copy-start.64
  96.4 12.2 %copy-start.9 = (f32[128,2048]{1,0:T(8,128)}, f32[128,2048]{1,0:T(8,128)S(1)}, u32[]{:S(2)}) copy-start(f32[128,2048]{1,0:T(8,128)S(1)} %fusion.36) | copy-start | bytes 3145732
  100.2 5.9 %copy-start.66 = (s32[128]{0:T(128)S(1)}, s32[128]{0:T(128)}, u32[]{:S(2)}) copy-start(s32[128]{0:T(128)} %param.16) | copy-start | bytes 1540
  101.0 5.4 %copy-start.61 = (f32[64]{0:T(128)}, f32[64]{0:T(128)S(1)}, u32[]{:S(2)}) copy-start(f32[64]{0:T(128)S(1)} %reshape.728) | copy-start | bytes 772
  110.4 3.1 copy-start.41
  112.0 2.4 copy-start.45
  112.0 2.4 copy-start.47
  113.8 6.0 %copy-start.67 = (s32[128]{0:T(128)S(1)}, s32[128]{0:T(128)}, u32[]{:S(2)}) copy-start(s32[128]{0:T(128)} %param.16) | copy-start | bytes 1540
  113.8 6.1 %copy-start.32 = (bf16[128,1024]{1,0:T(8,128)(2,1)S(1)}, bf16[128,1024]{1,0:T(8,128)(2,1)}, u32[]{:S(2)}) copy-start(bf16[128,1024]{1,0:T(8,128)(2,1)} %param.15) | copy-start | bytes 786436
  114.4 36.6 %copy-start.7 = (f32[128,1024]{1,0:T(8,128)}, f32[128,1024]{1,0:T(8,128)S(1)}, u32[]{:S(2)}) copy-start(f32[128,1024]{1,0:T(8,128)S(1)} %get-tuple-element.77) | copy-start | bytes 1572868
  114.4 36.5 %copy-start.43 = (f32[1,2,4,128]{3,1,2,0:T(2,128)}, f32[1,2,4,128]{3,1,2,0:T(2,128)S(1)}, u32[]{:S(2)}) copy-start(f32[1,2,4,128]{3,1,2,0:T(2,128)S(1)} %copy.108) | copy-start | bytes 12292
  114.5 36.4 %copy-start.58 = (f32[128]{0:T(128)}, f32[128]{0:T(128)S(1)}, u32[]{:S(2)}) copy-start(f32[128]{0:T(128)S(1)} %add_rsqrt_fusion.2) | copy-start | bytes 1540
  114.5 6.8 %copy-start.12 = (bf16[4,1152,1024]{2,1,0:T(8,128)(2,1)S(1)}, bf16[4,1152,1024]{2,1,0:T(8,128)(2,1)}, u32[]{:S(2)}) copy-start(bf16[4,1152,1024]{2,1,0:T(8,128)(2,1)} %get-tuple-element.30) | copy-start | bytes 28311556
  114.5 11.4 %slice-start.3 = ((s8[9437184]{0:T(1024)(128)(4,1)}), s8[4194304]{0:T(1024)(128)(4,1)S(1)}, s32[]{:S(2)}) async-start(s8[9437184]{0:T(1024)(128)(4,1)} %bitcast.174), calls=%async_computation.3 | async-start | bytes 8388608
  114.5 11.4 %slice-start.4 = ((s8[9437184]{0:T(1024)(128)(4,1)}), s8[4194304]{0:T(1024)(128)(4,1)S(1)}, s32[]{:S(2)}) async-start(s8[9437184]{0:T(1024)(128)(4,1)} %bitcast.174), calls=%async_computation.4 | async-start | bytes 8388608
  119.9 11.6 %copy-start.11 = (f32[128,4608]{1,0:T(8,128)}, f32[128,4608]{1,0:T(8,128)S(1)}, u32[]{:S(2)}) copy-start(f32[128,4608]{1,0:T(8,128)S(1)} %fusion.61) | copy-start | bytes 7077892
  121.3 4.7 %slice-start.5 = ((s8[9437184]{0:T(1024)(128)(4,1)}), s8[1048576]{0:T(1024)(128)(4,1)S(1)}, s32[]{:S(2)}) async-start(s8[9437184]{0:T(1024)(128)(4,1)} %bitcast.174), calls=%async_computation.5 | async-start | bytes 2097152
  126.0 21.3 %slice-start = ((s8[9437184]{0:T(1024)(128)(4,1)}), s8[4194304]{0:T(1024)(128)(4,1)S(1)}, s32[]{:S(2)}) async-start(s8[9437184]{0:T(1024)(128)(4,1)} %bitcast.169), calls=%async_computation | async-start | bytes 8388608
  131.4 6.9 %copy-start.13 = (f32[128,4608]{1,0:T(8,128)}, f32[128,4608]{1,0:T(8,128)S(1)}, u32[]{:S(2)}) copy-start(f32[128,4608]{1,0:T(8,128)S(1)} %get-tuple-element.78) | copy-start | bytes 7077892
  131.4 15.8 %slice-start.1 = ((s8[9437184]{0:T(1024)(128)(4,1)}), s8[4194304]{0:T(1024)(128)(4,1)S(1)}, s32[]{:S(2)}) async-start(s8[9437184]{0:T(1024)(128)(4,1)} %bitcast.169), calls=%async_computation.1 | async-start | bytes 8388608
  131.4 15.8 %slice-start.2 = ((s8[9437184]{0:T(1024)(128)(4,1)}), s8[1048576]{0:T(1024)(128)(4,1)S(1)}, s32[]{:S(2)}) async-start(s8[9437184]{0:T(1024)(128)(4,1)} %bitcast.169), calls=%async_computation.2 | async-start | bytes 2097152
  138.4 5.5 %copy-start.14 = (f32[128,4608]{1,0:T(8,128)S(1)}, f32[128,4608]{1,0:T(8,128)}, u32[]{:S(2)}) copy-start(f32[128,4608]{1,0:T(8,128)} %copy-done.13) | copy-start | bytes 7077892
  143.8 3.4 copy-start.35
  153.5 3.9 copy-start.42
  153.5 3.9 copy-start.50
  157.4 3.2 copy-start.19
  159.3 3.4 copy-start.56
  160.3 2.5 copy-start.22
  160.6 4.5 %copy-start.24 = (f32[128,512]{0,1:T(8,128)S(1)}, f32[128,512]{0,1:T(8,128)}, u32[]{:S(2)}) copy-start(f32[128,512]{0,1:T(8,128)} %copy-done.23) | copy-start | bytes 786436
  162.8 4.9 %copy-start.28 = (f32[128,512]{1,0:T(8,128)}, f32[128,512]{1,0:T(8,128)S(1)}, u32[]{:S(2)}) copy-start(f32[128,512]{1,0:T(8,128)S(1)} %copy.87) | copy-start | bytes 786436
  162.8 4.9 %copy-start.36 = (bf16[128,512]{1,0:T(8,128)(2,1)S(1)}, bf16[128,512]{1,0:T(8,128)(2,1)}, u32[]{:S(2)}) copy-start(bf16[128,512]{1,0:T(8,128)(2,1)} %copy.89) | copy-start | bytes 393220
  164.2 3.5 copy-start.37
  167.7 3.8 copy-start.54
  167.7 3.8 copy-start.65
  167.7 4.8 %copy-start.16 = (f32[128,1024]{1,0:T(8,128)S(1)}, f32[128,1024]{1,0:T(8,128)}, u32[]{:S(2)}) copy-start(f32[128,1024]{1,0:T(8,128)} %copy-done.15) | copy-start | bytes 1572868
  171.5 4.0 copy-start.8
  171.5 4.0 copy-start.44
  171.6 4.0 copy-start.59
  180.8 2.4 copy-start.34
  183.2 4.3 copy-start.29
  183.2 4.3 copy-start.31
  183.2 4.6 %copy-start.20 = (f32[128,1024]{1,0:T(8,128)S(1)}, f32[128,1024]{1,0:T(8,128)}, u32[]{:S(2)}) copy-start(f32[128,1024]{1,0:T(8,128)} %copy-done.19) | copy-start | bytes 1572868
  429.0 3.2 copy-start.27
  430.0 2.5 copy-start.26
  432.5 5.3 %copy-start.25 = (bf16[9,4,32,1024]{3,2,1,0:T(8,128)(2,1)S(1)}, bf16[9,4,32,1024]{3,2,1,0:T(8,128)(2,1)}, u32[]{:S(2)}) copy-start(bf16[9,4,32,1024]{3,2,1,0:T(8,128)(2,1)} %get-tuple-element.35) | copy-start | bytes 7077892
  437.8 2.9 copy-start.60
  (26 other events, 32.0 us)

commit v2 on v1

--- a/solution.py
+++ b/solution.py
@@ -292,6 +292,11 @@
     n_half = n_shard // 2
     steps = [("shard", i) for i in reversed(range(1, s_bits))] + [("rep", i) for i in range(r_bits)]
     back = [("rep", i) for i in reversed(range(r_bits))]
+    turned = list(steps)
+    if r_bits >= 2:
+        turned = [("rep", 1)] + [st for st in steps if st != ("rep", 1)]
+    turned_back = [st for st in reversed(turned) if st[0] == "rep"]
+    cycle = cfg["cycle"]
     n_down_steps, n_back = len(steps), len(back)
     ltf, rf, dsend = scratch[:3]
     recv = scratch[3 : 3 + n_down_steps]
@@ -307,6 +312,19 @@
 
     def peer(axis, bit):
         return {axis: (me_s if axis == "shard" else me_r) ^ (1 << bit)}
+
+    def is_turned(k):
+        return k % cycle == cycle // 2
+
+    def bit_at(i, k):
+        return jnp.where(is_turned(k), bit_of(*turned[i]), bit_of(*steps[i]))
+
+    def peer_at(first, second, k):
+        def moved(axis, me):
+            ids = [me ^ (1 << bit) if name == axis else me for name, bit in (first, second)]
+            return ids[0] if first == second else jnp.where(is_turned(k), ids[1], ids[0])
+
+        return {"rep": moved("rep", me_r), "shard": moved("shard", me_s)}
 
     everyone = [("shard", i) for i in range(s_bits)] + [("rep", i) for i in range(r_bits)]
     barrier = pltpu.get_barrier_semaphore()
@@ -372,33 +390,42 @@
     nb = n_half // 2
     top = bit_of(*steps[0])
 
+    def part_of(i, k, mine):
+        if r_bits < 2:
+            lead = top if mine else 1 - top
+            return product(lead * nb + i // 2, k, i % 2)
+        turn, z = is_turned(k), bit_of(*turned[0])
+        lead, half = (top, z) if mine else (1 - top, 1 - z)
+        return product(jnp.where(turn, i, lead * nb + i // 2), k, jnp.where(turn, half, i % 2))
+
     def rs_copy(i, k):
-        axis, bit = steps[i]
         if i == 0:
             src = dsend.at[k % slots]
         else:
             half = recv[i - 1].shape[1] // 2
-            src = recv[i - 1].at[k, pl.ds((1 - bit_of(axis, bit)) * half, half)]
+            src = recv[i - 1].at[k, pl.ds((1 - bit_at(i, k)) * half, half)]
         return pltpu.make_async_remote_copy(
             src_ref=src, dst_ref=recv[i].at[k], send_sem=send_sem.at[i, k], recv_sem=recv_sem.at[i, k],
-            device_id=peer(axis, bit), device_id_type=MESH)
-
-    def own_start(size):
-        at = 0
-        for n, (axis, bit) in enumerate(steps[s_bits - 1 :]):
-            block = n_rep >> (n + 1)
-            if block >= size:
-                at = at + bit_of(axis, bit) * block
-        return at
+            device_id=peer_at(steps[i], turned[i], k), device_id_type=MESH)
+
+    def own_start(size, k):
+        def start(order):
+            at = 0
+            for n, (axis, bit) in enumerate(order):
+                block = n_rep >> (n + 1)
+                if block >= size:
+                    at = at + bit_of(axis, bit) * block
+            return at
+
+        return jnp.where(is_turned(k), start(turned_back[::-1]), start(back[::-1]))
 
     def ag_copy(i, k):
-        axis, bit = back[i]
         size = 1 << i
-        at = pl.ds(own_start(size), size)
+        at = pl.ds(own_start(size, k), size)
         n = n_down_steps + i
         return pltpu.make_async_remote_copy(
             src_ref=outb.at[k, at], dst_ref=outb.at[k, at], send_sem=send_sem.at[n, k], recv_sem=recv_sem.at[n, k],
-            device_id=peer(axis, bit), device_id_type=MESH)
+            device_id=peer_at(back[i], turned_back[i], k), device_id_type=MESH)
 
     def out_copies(n, k):
         lo = cfg["sets"][n][0]
@@ -424,31 +451,32 @@
                 for cp in out_copies(n, k):
                     act(cp)
 
+    def spread(i):
+        for p, a, b in pieces(0):
+            yield i * (n_rep // 2) + p, a, b
+
     def first(k):
-        for i in range(nb):
-            for j in range(2):
-                part = product((1 - top) * nb + i, k, j).astype(jnp.bfloat16)
-                for p, a, b in pieces(j):
-                    dsend[k % slots, i * n_rep + p] = part[a : a + pr, b : b + pc]
+        for i in range(n_half):
+            part = part_of(i, k, False).astype(jnp.bfloat16)
+            for q, a, b in spread(i):
+                dsend[k % slots, q] = part[a : a + pr, b : b + pc]
 
     def join(i, k):
         rs_copy(i, k).wait()
         if i == 0:
-            for n in range(nb):
-                for j in range(2):
-                    part = product(top * nb + n, k, j)
-                    for p, a, b in pieces(j):
-                        q = n * n_rep + p
-                        got = recv[0][k, q].astype(jnp.float32)
-                        recv[0][k, q] = (part[a : a + pr, b : b + pc] + got).astype(jnp.bfloat16)
+            for n in range(n_half):
+                part = part_of(n, k, True)
+                for q, a, b in spread(n):
+                    got = recv[0][k, q].astype(jnp.float32)
+                    recv[0][k, q] = (part[a : a + pr, b : b + pc] + got).astype(jnp.bfloat16)
             return
         half = recv[i].shape[1]
-        base = bit_of(*steps[i]) * half
+        base = bit_at(i, k) * half
         for q in range(half):
             kept = recv[i - 1][k, base + q].astype(jnp.float32)
             both = (kept + recv[i][k, q].astype(jnp.float32)).astype(jnp.bfloat16)
             if i == n_down_steps - 1:
-                outb[k, own_start(1)] = both
+                outb[k, own_start(1, k)] = both
             else:
                 recv[i][k, q] = both
 
@@ -523,7 +551,7 @@
     right = jnp.concatenate([dyb, dgate, dup, dqkv, dx2b], axis=1)
     lrows, rcols = lt.shape[2], right.shape[1]
     cfg = dict(
-        n_rep=n_rep, n_shard=n_shard, tok=tok, sub=sub, cols=cols, pr=pr, pc=pc, depth=depth,
+        n_rep=n_rep, n_shard=n_shard, tok=tok, sub=sub, cols=cols, pr=pr, pc=pc, depth=depth, cycle=6,
         n_down=n_down, n_mid=n_mid, n_qkv=n_qkv, n_all=n_all, lout=fs + 2 * ds,
         lsegs=((0, fs), (fs, fs + ds), (fs + ds, lrows)),
         rsegs=((0, depth), (depth, depth + 2 * ff), (depth + 2 * ff, rcols)),

time: 443 us -> 438 us (0.989)
  Pallas kernels: 321 us -> 315 us
    pallas_call x1, Pallas kernels: 239 us -> 233 us  [reduce_grads(): pl.pallas_call(functools.partial(sum_kernel, cfg), name='sum_grads', out_...]
where the time goes in v2:
time: 438 us; the launch traced here: 436 us
  Pallas kernels  315 us (72%)
  matrix products  45.1 us (10%)
  other arithmetic  39.3 us (9%)
  local copies, waits for them, and re-layouts  35.3 us (8%)
    pallas_call x1, Pallas kernels, reduce_grads(): pl.pallas_call(functools.partial(sum_kernel, cfg), name='sum_grads', out_...  233 us
    pallas_call x1, Pallas kernels, gather_all(): pl.pallas_call(functools.partial(gather_kernel, {'items': items, 'n_in':...  82.2 us
    dot_general x5, matrix products, matmul(): return jnp.dot(left, right, preferred_element_type=jnp.float32)  21.2 us
    dot_general x5, matrix products, matmul_t(): lax.dot_general(left, right, (((1,), (1,)), ((), ())), preferred_element_...  19.1 us
    unnamed x152, local copies, waits for them, and re-layouts  12.1 us
    convert_element_type x4, other arithmetic, reduce_grads(): v.reshape(-1, v.shape[-1]).astype(jnp.float32)  10.7 us

profile of v2, /device:TPU:0, one launch (start us, length us, event | category | flops | bytes accessed | tf_op | source)
XLA Modules:
  0.0 436.5 jit_solution(14273165621876215531)
XLA Ops:
  1.4 1.7 copy-done
  3.1 1.7 copy-done.1
  4.8 1.7 copy-done.2
  6.4 1.0 copy-done.3
  7.5 1.0 copy-done.4
  8.5 0.9 copy-done.5
  9.5 0.9 copy-done.6
  10.4 82.2 %gather_weights.1 = (bf16[4,256,2048]{2,1,0:T(8,128)(2,1)}, bf16[4,256,1024]{2,1,0:T(8,128)(2,1)S(1)}, bf16[4,256,4608]{2,1,0:T(8,128)(2,1)}, bf16[4,256,4608]{2...) custom-call(bf16[256,1024]{1,0:T(8,128)(2,1)S(1)} %copy-done.3, ...), custom_call_target="tpu_custom_call" | custom-call | tf_op jit(solution)/shard_map/gather_weights/pallas_call | solution.py:268
  93.4 3.0 fusion.36
  97.1 1.0 copy.73
  98.1 1.4 fusion.40
  101.0 0.8 slice.104
  101.8 2.0 copy.75
  103.9 1.1 multiply_reduce_fusion.6
  105.0 1.2 multiply_multiply_fusion
  107.3 1.3 reshape.727
  109.3 1.1 copy.74
  112.0 1.4 select_reduce_fusion
  114.6 5.3 %fusion.61 = f32[128,4608]{1,0:T(8,128)S(1)} fusion(bf16[1024,4608]{1,0:T(8,128)(2,1)} %bitcast.168, f32[128,1024]{1,0:T(8,128)S(1)} %get-tuple-element.77, f32[1024]{0:T(1024)S(1)} %bitcast.203, f32[128]{0:T(128)S(1)} %add_rsqrt_fusion.2), kind=kOutput, calls=%fused_computation.145 | convolution fusion | flops 1208352768 | bytes 12325376 | tf_op jit(solution)/shard_map/dot_general | solution.py:23
  119.9 0.8 fusion.31
  121.3 4.7 %fusion.32 = f32[128,4608]{1,0:T(8,128)} fusion(bf16[4608,1024]{1,0:T(8,128)(2,1)S(1)} %bitcast.179, bf16[128,1024]{1,0:T(8,128)(2,1)S(1)} %copy-done.32, f32[128]{0:T(128)S(1)} %compare_convert_fusion), kind=kOutput, calls=%fused_computation.89 | convolution fusion | flops 1208352768 | bytes 12059136 | tf_op jit(solution)/shard_map/dot_general | solution.py:27
  126.0 5.4 %constant_dynamic-update-slice_fusion.4 = (bf16[128,13312]{1,0:T(8,128)(2,1)}, bf16[128,4608]{1,0:T(8,128)(2,1)}, f32[128,4608]{1,0:T(8,128)S(1)}) fusion(bf16[128,13312]{1,0:T(8,128)(2,1)} %fusion.31, f32[128,4608]{1,0:T(8,128)} %fusion.32, f32[128,4608]{1,0:T(8,128)S(1)} %fusion.61, bf16[1024,4608]{1,0:T(8,128)(2,1)S(1)} %bitcast.176, ...), kind=kOutput, calls=%fused_computation.107 | convolution fusion | flops 1214251008 | bytes 19403264 | tf_op jit(solution)/shard_map/dot_general | solution.py:23
  131.4 6.9 %fusion.6 = bf16[128,1024]{1,0:T(8,128)(2,1)} fusion(f32[128,1024]{1,0:T(8,128)S(1)} %get-tuple-element.77, bf16[4608,1024]{1,0:T(8,128)(2,1)} %bitcast.178, f32[128,4608]{1,0:T(8,128)S(1)} %fusion.61, f32[128,4608]{1,0:T(8,128)S(1)} %get-tuple-element.78), kind=kOutput, calls=%fused_computation.22 | convolution fusion | flops 1211760640 | bytes 14942208 | tf_op jit(solution)/shard_map/dot_general | solution.py:23
  138.4 5.5 %fusion.62 = f32[128,1024]{1,0:T(8,128)} fusion(bf16[128,4608]{1,0:T(8,128)(2,1)} %get-tuple-element.48, bf16[1024,4608]{1,0:T(8,128)(2,1)S(1)} %bitcast.177), kind=kOutput, calls=%fused_computation.146 | convolution fusion | flops 1207959552 | bytes 11141120 | tf_op jit(solution)/shard_map/dot_general | solution.py:27
  143.8 3.4 constant_dynamic-update-slice_fusion.3
  147.3 3.7 multiply_reduce_fusion.2
  152.0 1.5 convolution_convert_fusion
  153.5 1.1 copy.77
  154.7 1.0 fusion.7
  159.3 1.0 copy.81
  160.6 2.1 constant_dynamic-update-slice_fusion.2
  162.9 1.4 convolution_bitcast_fusion.2
  167.7 3.8 fusion.22
  171.6 0.9 fusion.19
  172.5 1.0 fusion.18
  173.5 1.1 concatenate.97
  174.7 0.9 copy.93
  175.9 0.9 copy.92
  176.8 4.0 fusion
  180.8 2.4 copy.90
  183.2 2.9 maximum_bitcast_fusion.lt_ref
  189.0 233.0 %sum_grads.1 = (bf16[9,4,32,1024]{3,2,1,0:T(8,128)(2,1)}, bf16[8,32,4608]{2,1,0:T(8,128)(2,1)}, bf16[8,32,4608]{2,1,0:T(8,128)(2,1)}, bf16[8,32,2048]{2,1,0:T(8,...) custom-call(bf16[2,2,1920,128]{3,2,1,0:T(8,128)(2,1)} %maximum_bitcast_fusion.lt_ref, ...), custom_call_target="tpu_custom_call" | custom-call | tf_op jit(solution)/shard_map/sum_grads/pallas_call | solution.py:571
  422.0 1.5 bitcast_convert_fusion.3
  423.5 1.0 split.12
  424.5 1.0 fusion.59
  425.5 1.1 bitcast_convert_fusion.4
  427.0 5.3 %bitcast_convert_fusion.1 = (f32[256,4608]{1,0:T(8,128)}, f32[256,4608]{1,0:T(8,128)}) fusion(bf16[8,32,4608]{2,1,0:T(8,128)(2,1)S(1)} %copy-done.27, bf16[8,32,4608]{2,1,0:T(8,128)(2,1)S(1)} %copy-done.26), kind=kLoop, calls=%fused_computation.1 | loop fusion | flops 2359296 | bytes 14155776 | tf_op jit(solution)/shard_map/convert_element_type | solution.py:596
  432.3 2.9 bitcast_convert_fusion
  (216 shorter events, 21.8 us)
Async XLA Ops:
  10.4 82.8 %copy-start.18 = (bf16[128,1024]{1,0:T(8,128)(2,1)S(1)}, bf16[128,1024]{1,0:T(8,128)(2,1)}, u32[]{:S(2)}) copy-start(bf16[128,1024]{1,0:T(8,128)(2,1)} %param.14) | copy-start | bytes 786436
  93.2 3.1 copy-start.53
  93.4 3.0 copy-start.64
  96.4 12.2 %copy-start.9 = (f32[128,2048]{1,0:T(8,128)}, f32[128,2048]{1,0:T(8,128)S(1)}, u32[]{:S(2)}) copy-start(f32[128,2048]{1,0:T(8,128)S(1)} %fusion.36) | copy-start | bytes 3145732
  100.2 5.9 %copy-start.66 = (s32[128]{0:T(128)S(1)}, s32[128]{0:T(128)}, u32[]{:S(2)}) copy-start(s32[128]{0:T(128)} %param.16) | copy-start | bytes 1540
  101.0 5.4 %copy-start.61 = (f32[64]{0:T(128)}, f32[64]{0:T(128)S(1)}, u32[]{:S(2)}) copy-start(f32[64]{0:T(128)S(1)} %reshape.728) | copy-start | bytes 772
  110.4 3.1 copy-start.41
  112.0 2.4 copy-start.45
  112.0 2.4 copy-start.47
  113.8 6.0 %copy-start.67 = (s32[128]{0:T(128)S(1)}, s32[128]{0:T(128)}, u32[]{:S(2)}) copy-start(s32[128]{0:T(128)} %param.16) | copy-start | bytes 1540
  113.8 6.1 %copy-start.32 = (bf16[128,1024]{1,0:T(8,128)(2,1)S(1)}, bf16[128,1024]{1,0:T(8,128)(2,1)}, u32[]{:S(2)}) copy-start(bf16[128,1024]{1,0:T(8,128)(2,1)} %param.15) | copy-start | bytes 786436
  114.4 36.6 %copy-start.7 = (f32[128,1024]{1,0:T(8,128)}, f32[128,1024]{1,0:T(8,128)S(1)}, u32[]{:S(2)}) copy-start(f32[128,1024]{1,0:T(8,128)S(1)} %get-tuple-element.77) | copy-start | bytes 1572868
  114.4 36.5 %copy-start.43 = (f32[1,2,4,128]{3,1,2,0:T(2,128)}, f32[1,2,4,128]{3,1,2,0:T(2,128)S(1)}, u32[]{:S(2)}) copy-start(f32[1,2,4,128]{3,1,2,0:T(2,128)S(1)} %copy.108) | copy-start | bytes 12292
  114.5 36.4 %copy-start.58 = (f32[128]{0:T(128)}, f32[128]{0:T(128)S(1)}, u32[]{:S(2)}) copy-start(f32[128]{0:T(128)S(1)} %add_rsqrt_fusion.2) | copy-start | bytes 1540
  114.5 6.8 %copy-start.12 = (bf16[4,1152,1024]{2,1,0:T(8,128)(2,1)S(1)}, bf16[4,1152,1024]{2,1,0:T(8,128)(2,1)}, u32[]{:S(2)}) copy-start(bf16[4,1152,1024]{2,1,0:T(8,128)(2,1)} %get-tuple-element.30) | copy-start | bytes 28311556
  114.5 11.4 %slice-start.3 = ((s8[9437184]{0:T(1024)(128)(4,1)}), s8[4194304]{0:T(1024)(128)(4,1)S(1)}, s32[]{:S(2)}) async-start(s8[9437184]{0:T(1024)(128)(4,1)} %bitcast.174), calls=%async_computation.3 | async-start | bytes 8388608
  114.5 11.4 %slice-start.4 = ((s8[9437184]{0:T(1024)(128)(4,1)}), s8[4194304]{0:T(1024)(128)(4,1)S(1)}, s32[]{:S(2)}) async-start(s8[9437184]{0:T(1024)(128)(4,1)} %bitcast.174), calls=%async_computation.4 | async-start | bytes 8388608
  119.9 11.6 %copy-start.11 = (f32[128,4608]{1,0:T(8,128)}, f32[128,4608]{1,0:T(8,128)S(1)}, u32[]{:S(2)}) copy-start(f32[128,4608]{1,0:T(8,128)S(1)} %fusion.61) | copy-start | bytes 7077892
  121.3 4.7 %slice-start.5 = ((s8[9437184]{0:T(1024)(128)(4,1)}), s8[1048576]{0:T(1024)(128)(4,1)S(1)}, s32[]{:S(2)}) async-start(s8[9437184]{0:T(1024)(128)(4,1)} %bitcast.174), calls=%async_computation.5 | async-start | bytes 2097152
  126.0 21.3 %slice-start = ((s8[9437184]{0:T(1024)(128)(4,1)}), s8[4194304]{0:T(1024)(128)(4,1)S(1)}, s32[]{:S(2)}) async-start(s8[9437184]{0:T(1024)(128)(4,1)} %bitcast.169), calls=%async_computation | async-start | bytes 8388608
  131.4 6.9 %copy-start.13 = (f32[128,4608]{1,0:T(8,128)}, f32[128,4608]{1,0:T(8,128)S(1)}, u32[]{:S(2)}) copy-start(f32[128,4608]{1,0:T(8,128)S(1)} %get-tuple-element.78) | copy-start | bytes 7077892
  131.4 15.8 %slice-start.1 = ((s8[9437184]{0:T(1024)(128)(4,1)}), s8[4194304]{0:T(1024)(128)(4,1)S(1)}, s32[]{:S(2)}) async-start(s8[9437184]{0:T(1024)(128)(4,1)} %bitcast.169), calls=%async_computation.1 | async-start | bytes 8388608
  131.4 15.8 %slice-start.2 = ((s8[9437184]{0:T(1024)(128)(4,1)}), s8[1048576]{0:T(1024)(128)(4,1)S(1)}, s32[]{:S(2)}) async-start(s8[9437184]{0:T(1024)(128)(4,1)} %bitcast.169), calls=%async_computation.2 | async-start | bytes 2097152
  138.4 5.5 %copy-start.14 = (f32[128,4608]{1,0:T(8,128)S(1)}, f32[128,4608]{1,0:T(8,128)}, u32[]{:S(2)}) copy-start(f32[128,4608]{1,0:T(8,128)} %copy-done.13) | copy-start | bytes 7077892
  143.8 3.4 copy-start.35
  153.5 3.9 copy-start.42
  153.5 3.9 copy-start.50
  157.4 3.2 copy-start.19
  159.3 3.4 copy-start.56
  160.3 2.5 copy-start.22
  160.6 4.5 %copy-start.24 = (f32[128,512]{0,1:T(8,128)S(1)}, f32[128,512]{0,1:T(8,128)}, u32[]{:S(2)}) copy-start(f32[128,512]{0,1:T(8,128)} %copy-done.23) | copy-start | bytes 786436
  162.8 4.9 %copy-start.28 = (f32[128,512]{1,0:T(8,128)}, f32[128,512]{1,0:T(8,128)S(1)}, u32[]{:S(2)}) copy-start(f32[128,512]{1,0:T(8,128)S(1)} %copy.87) | copy-start | bytes 786436
  162.8 4.9 %copy-start.36 = (bf16[128,512]{1,0:T(8,128)(2,1)S(1)}, bf16[128,512]{1,0:T(8,128)(2,1)}, u32[]{:S(2)}) copy-start(bf16[128,512]{1,0:T(8,128)(2,1)} %copy.89) | copy-start | bytes 393220
  164.2 3.5 copy-start.37
  167.7 3.8 copy-start.54
  167.7 3.8 copy-start.65
  167.7 4.8 %copy-start.16 = (f32[128,1024]{1,0:T(8,128)S(1)}, f32[128,1024]{1,0:T(8,128)}, u32[]{:S(2)}) copy-start(f32[128,1024]{1,0:T(8,128)} %copy-done.15) | copy-start | bytes 1572868
  171.5 4.0 copy-start.8
  171.5 4.0 copy-start.44
  171.6 4.0 copy-start.59
  180.8 2.4 copy-start.34
  183.2 4.3 copy-start.29
  183.2 4.3 copy-start.31
  183.2 4.6 %copy-start.20 = (f32[128,1024]{1,0:T(8,128)S(1)}, f32[128,1024]{1,0:T(8,128)}, u32[]{:S(2)}) copy-start(f32[128,1024]{1,0:T(8,128)} %copy-done.19) | copy-start | bytes 1572868
  423.4 3.2 copy-start.27
  424.5 2.5 copy-start.26
  427.0 5.3 %copy-start.25 = (bf16[9,4,32,1024]{3,2,1,0:T(8,128)(2,1)S(1)}, bf16[9,4,32,1024]{3,2,1,0:T(8,128)(2,1)}, u32[]{:S(2)}) copy-start(bf16[9,4,32,1024]{3,2,1,0:T(8,128)(2,1)} %get-tuple-element.35) | copy-start | bytes 7077892
  432.3 2.9 copy-start.60
  (26 other events, 32.0 us)

commit v3 on v2

--- a/solution.py
+++ b/solution.py
@@ -276,12 +276,15 @@
             dma((n, 11)), dma((n, 11)), dma((n,)), dma((n, 4)), dma((3,)), dma((3,)), dma,
         ],
         compiler_params=pltpu.CompilerParams(
-            collective_id=1, has_side_effects=True, vmem_limit_bytes=44_000_000),
+            collective_id=1, has_side_effects=True, vmem_limit_bytes=65_000_000),
     )(*ins, gains)
     return [g.reshape(-1, g.shape[-1]) for g in got[:-1]], got[-1]
 
 
-def sum_kernel(cfg, lt_ref, r_ref, g_ref, *refs):
+def sum_kernel(cfg, *refs):
+    n_left, n_right = cfg["n_left"], cfg["n_right"]
+    left_refs, right_refs = refs[:n_left], refs[n_left : n_left + n_right]
+    g_ref, refs = refs[n_left + n_right], refs[n_left + n_right + 1 :]
     n_sets = len(cfg["sets"])
     out_refs, gout_ref, scratch = refs[:n_sets], refs[n_sets], refs[n_sets + 1 :]
     n_rep, n_shard, tok = cfg["n_rep"], cfg["n_shard"], cfg["tok"]
@@ -333,27 +336,29 @@
     pl.semaphore_wait(barrier, len(everyone))
 
     def exchange(i):
-        (l0, l1), (r0, r1) = lsegs[i], rsegs[i]
-        remote = [
-            pltpu.make_async_remote_copy(
-                src_ref=lt_ref.at[1 - core, :, pl.ds(l0, l1 - l0)],
-                dst_ref=ltf.at[:, pl.ds(l0, l1 - l0), pl.ds(tok, tok)],
-                send_sem=ex_send.at[i, 0], recv_sem=ex_recv.at[i, 0],
-                device_id=peer("shard", 0), device_id_type=MESH),
-            pltpu.make_async_remote_copy(
-                src_ref=r_ref.at[:, pl.ds(r0, r1 - r0)],
-                dst_ref=rf.at[pl.ds(tok, tok), pl.ds(r0, r1 - r0)],
-                send_sem=ex_send.at[i, 1], recv_sem=ex_recv.at[i, 1],
-                device_id=peer("shard", 0), device_id_type=MESH),
-        ]
-        local = [
-            pltpu.make_async_copy(
-                lt_ref.at[core, :, pl.ds(l0, l1 - l0)],
-                ltf.at[:, pl.ds(l0, l1 - l0), pl.ds(0, tok)], ex_own.at[i, 0]),
-            pltpu.make_async_copy(
-                r_ref.at[:, pl.ds(r0, r1 - r0)], rf.at[pl.ds(0, tok), pl.ds(r0, r1 - r0)], ex_own.at[i, 1]),
-        ]
-        return remote + local
+        made, n = [], 0
+        for which, refs_of, span, target in ((0, left_refs, lsegs[i], ltf), (1, right_refs, rsegs[i], rf)):
+            at = 0
+            for ref in refs_of:
+                size = ref.shape[1] // n_shard if which == 0 else ref.shape[1]
+                if span[0] <= at < span[1]:
+                    for half in range(n_half if which == 0 else 1):
+                        def source(c):
+                            first = pl.multiple_of((half * 2 + c) * size, size)
+                            return ref.at[:, pl.ds(first, size)] if which == 0 else ref
+
+                        def place_at(row):
+                            held = target.at[half] if which == 0 else target
+                            return held.at[pl.ds(row, tok), pl.ds(at, size)]
+
+                        made.append(pltpu.make_async_remote_copy(
+                            src_ref=source(1 - core), dst_ref=place_at(tok),
+                            send_sem=ex_send.at[i, n], recv_sem=ex_recv.at[i, n],
+                            device_id=peer("shard", 0), device_id_type=MESH))
+                        made.append(pltpu.make_async_copy(source(core), place_at(0), ex_own.at[i, n]))
+                        n += 1
+                at += size
+        return made
 
     for i in range(3):
         for cp in exchange(i):
@@ -377,8 +382,9 @@
 
     def product(blk, k, j):
         lrow, rcol = place(k, j)
-        return jnp.dot(
-            ltf[blk, pl.ds(lrow, sub), :], rf[:, pl.ds(rcol, cols)], preferred_element_type=jnp.float32)
+        return lax.dot_general(
+            ltf[blk, :, pl.ds(lrow, sub)], rf[:, pl.ds(rcol, cols)], (((0,), (0,)), ((), ())),
+            preferred_element_type=jnp.float32)
 
     rows_p, cols_p = sub // pr, cols // pc
 
@@ -534,24 +540,36 @@
     gout.wait()
 
 
+def plain_sums(pairs, gains):
+    sums = []
+    for left, right in pairs:
+        part = lax.dot_general(left, right, (((0,), (0,)), ((), ())), preferred_element_type=jnp.float32)
+        part = part.astype(jnp.bfloat16).astype(jnp.float32)
+        part = lax.psum_scatter(part, "shard", scatter_dimension=0, tiled=True)
+        sums.append(lax.psum(part, "rep"))
+    return sums, lax.psum(gains, ("rep", "shard"))
+
+
 def reduce_grads(hid, h2, h1, ob, dyb, dgate, dup, dqkv, dx2b, gains, n_rep, n_shard):
     tok, ff = hid.shape
     depth = h1.shape[1]
     qkv = dqkv.shape[1]
     n_half = n_shard // 2
     sub = depth // n_shard // 2
+    if n_shard < 4 or sub % 128 or ff // n_shard % 128:
+        pairs = ((hid, dyb), (h2, dgate), (h2, dup), (h1, dqkv), (ob, dx2b))
+        return plain_sums(pairs, gains)
     cols = depth // 2
     pr = max(16, 2 * sub // n_rep)
     pc = cols * (2 * sub // pr) // n_rep
     n_down, n_mid, n_qkv, n_out = ff // cols, 2 * ff // cols, qkv // cols, depth // cols
     n_all = n_down + n_mid + n_qkv + n_out
     fs, ds = ff // n_shard, depth // n_shard
-    lt = jnp.concatenate([v.T.reshape(n_shard, -1, tok) for v in (hid, h2, h1, ob)], axis=1)
-    lt = lt.reshape(n_half, 2, -1, tok).transpose(1, 0, 2, 3)
-    right = jnp.concatenate([dyb, dgate, dup, dqkv, dx2b], axis=1)
-    lrows, rcols = lt.shape[2], right.shape[1]
+    lefts, rights = (hid, h2, h1, ob), (dyb, dgate, dup, dqkv, dx2b)
+    lrows, rcols = sum(v.shape[1] // n_shard for v in lefts), sum(v.shape[1] for v in rights)
     cfg = dict(
-        n_rep=n_rep, n_shard=n_shard, tok=tok, sub=sub, cols=cols, pr=pr, pc=pc, depth=depth, cycle=6,
+        n_rep=n_rep, n_shard=n_shard, tok=tok, sub=sub, cols=cols, pr=pr, pc=pc, depth=depth, n_left=len(lefts), n_right=len(rights),
+        cycle=6,
         n_down=n_down, n_mid=n_mid, n_qkv=n_qkv, n_all=n_all, lout=fs + 2 * ds,
         lsegs=((0, fs), (fs, fs + ds), (fs + ds, lrows)),
         rsegs=((0, depth), (depth, depth + 2 * ff), (depth + 2 * ff, rcols)),
@@ -575,23 +593,23 @@
             *[jax.ShapeDtypeStruct(shape, bf) for shape in shapes],
             jax.ShapeDtypeStruct((g_rows, 128), jnp.float32),
         ),
-        in_specs=[pl.BlockSpec(memory_space=pltpu.VMEM)] * 3,
+        in_specs=[pl.BlockSpec(memory_space=pltpu.VMEM)] * (len(lefts) + len(rights) + 1),
         out_specs=[pl.BlockSpec(memory_space=pltpu.HBM)] * (len(shapes) + 1),
         scratch_shapes=[
-            pltpu.VMEM((n_half, lrows, 2 * tok), bf),
+            pltpu.VMEM((n_half, 2 * tok, lrows), bf),
             pltpu.VMEM((2 * tok, rcols), bf),
             pltpu.VMEM((slots, sizes[0], pr, pc), bf),
             *[pltpu.VMEM((n_all, size, pr, pc), bf) for size in sizes],
             pltpu.VMEM((n_all, n_rep, pr, pc), bf),
             pltpu.VMEM((n_hops + 1, g_rows, 128), jnp.float32),
             pltpu.VMEM((n_hops, g_rows, 128), jnp.float32),
-            dma((3, 2)), dma((3, 2)), dma((3, 2)),
+            *[dma((3, 2 * n_half + 4))] * 3,
             dma((n_steps + r_bits, n_all)), dma((n_steps + r_bits, n_all)), dma((n_all, 2 if cp == 1 else n_rep)),
             dma((n_hops,)), dma((n_hops,)), dma,
         ],
         compiler_params=pltpu.CompilerParams(
             collective_id=0, has_side_effects=True, vmem_limit_bytes=60_000_000),
-    )(lt, right, gains)
+    )(*lefts, *rights, gains)
 
     return [v.reshape(-1, v.shape[-1]).astype(jnp.float32) for v in outs], gsum
 

time: 438 us -> 421 us (0.961)
  other arithmetic: 39.3 us -> 25.5 us
  local copies, waits for them, and re-layouts: 35.3 us -> 25.9 us
  matrix products: 45.1 us -> 51.7 us
    unnamed x152 -> x131, local copies, waits for them, and re-layouts: 12.1 us -> 2.4 us
    dot_general x5, matrix products: 19.1 us -> 26.7 us  [matmul_t(): lax.dot_general(left, right, (((1,), (1,)), ((), ())), preferred_element_...]
    unnamed x7 -> x3, other arithmetic: 7.62 us -> 0.6 us
    mul x4, local copies, waits for them, and re-layouts: 1.07 us -> 6.09 us  [norm_rows(): normed = values * inv_rms]
where the time goes in v3:
time: 421 us; the launch traced here: 420 us
  Pallas kernels  316 us (75%)
  matrix products  51.7 us (12%)
  local copies, waits for them, and re-layouts  25.9 us (6%)
  other arithmetic  25.5 us (6%)
    pallas_call x1, Pallas kernels, reduce_grads(): pl.pallas_call(functools.partial(sum_kernel, cfg), name='sum_grads', out_...  233 us
    pallas_call x1, Pallas kernels, gather_all(): pl.pallas_call(functools.partial(gather_kernel, {'items': items, 'n_in':...  82.8 us
    dot_general x5, matrix products, matmul_t(): lax.dot_general(left, right, (((1,), (1,)), ((), ())), preferred_element_...  26.7 us
    dot_general x5, matrix products, matmul(): return jnp.dot(left, right, preferred_element_type=jnp.float32)  20.4 us
    convert_element_type x4, other arithmetic, reduce_grads(): v.reshape(-1, v.shape[-1]).astype(jnp.float32)  11.8 us

profile of v3, /device:TPU:0, one launch (start us, length us, event | category | flops | bytes accessed | tf_op | source)
XLA Modules:
  0.0 420.5 jit_solution(3999526724957084670)
XLA Ops:
  0.6 1.4 fusion.33.refs_7_
  2.0 82.8 %gather_weights.1 = (bf16[4,256,2048]{2,1,0:T(8,128)(2,1)}, bf16[4,256,1024]{2,1,0:T(8,128)(2,1)}, bf16[4,256,4608]{2,1,0:T(8,128)(2,1)}, bf16[4,256,4608]{2,1,0...) custom-call(bf16[256,1024]{1,0:T(8,128)(2,1)} %refs_0_.1, bf16[256,512]{1,0:T(8,128)(2,1)} %refs_1_.1, ...), custom_call_target="tpu_custom_call" | custom-call | tf_op jit(solution)/shard_map/gather_weights/pallas_call | solution.py:268
  84.8 0.7 copy.99
  85.6 0.6 convert_bitcast_fusion
  86.8 2.9 fusion.43
  90.8 0.7 fusion.20
  92.2 1.3 select_reduce_fusion
  94.1 2.2 multiply_reduce_fusion.5
  96.5 6.7 %fusion.45 = f32[128,4608]{1,0:T(8,128)} fusion(bf16[128,1024]{1,0:T(8,128)(2,1)S(1)} %multiply_convert_fusion.5.refs_1_, bf16[1024,4608]{1,0:T(8,128)(2,1)} %bitcast.137), kind=kOutput, calls=%fused_computation.123 | convolution fusion | flops 1207959552 | bytes 12058624 | tf_op jit(solution)/shard_map/dot_general | solution.py:23
  103.2 2.8 fusion.44
  106.2 9.8 %multiply_convert_fusion = (bf16[128,4608]{1,0:T(8,128)(2,1)S(1)}, bf16[128,4608]{1,0:T(8,128)(2,1)S(1)}, bf16[128,4608]{1,0:T(8,128)(2,1)}) fusion(f32[128,4608]{1,0:T(8,128)} %fusion.44, f32[128,4608]{1,0:T(8,128)} %fusion.45, bf16[128,1024]{1,0:T(8,128)(2,1)S(1)} %fusion.18.refs_4_, bf16[4608,1024]{1,0:T(8,128)(2,1)} %bitcast.145), kind=kOutput, calls=%fused_computation.3 | convolution fusion | flops 1216806912 | bytes 17956864 | tf_op jit(solution)/shard_map/dot_general | solution.py:27
  116.1 7.6 %fusion.46 = f32[128,1024]{1,0:T(8,128)S(1)} fusion(bf16[128,4608]{1,0:T(8,128)(2,1)S(1)} %get-tuple-element.44.refs_5_, bf16[1024,4608]{1,0:T(8,128)(2,1)} %bitcast.141), kind=kOutput, calls=%fused_computation.124 | convolution fusion | flops 1207959552 | bytes 11141120 | tf_op jit(solution)/shard_map/dot_general | solution.py:27
  123.8 3.9 multiply_reduce_fusion.2
  127.7 1.0 fusion.40
  128.7 0.7 copy-done.12
  129.4 1.5 convolution_convert_fusion
  131.0 1.1 copy.71
  132.2 1.3 multiply_reduce_fusion
  134.3 0.9 pad_maximum_fusion
  135.2 1.0 copy.75
  136.2 2.1 copy.73
  138.3 0.8 mul.566
  139.2 2.1 copy.76
  141.2 1.3 mul.575
  142.5 1.4 mul.576
  143.9 2.8 multiply_reduce_fusion.1
  147.1 0.7 pad_maximum_fusion.3
  147.9 0.7 mul.599
  148.6 1.8 copy.80
  150.4 1.8 copy.78
  152.2 1.4 mul.586
  153.6 1.8 copy.81
  155.4 0.7 mul.592
  156.2 1.2 multiply_reduce_fusion.7
  157.4 1.3 fusion.3
  158.8 3.8 fusion.15
  163.3 0.6 bitcast_convert_fusion.5.refs_9_
  163.9 0.8 pad_maximum_fusion.1.refs_7_
  164.7 0.8 copy.86.refs_3_
  165.6 232.8 %sum_grads.1 = (bf16[9,4,32,1024]{3,2,1,0:T(8,128)(2,1)}, bf16[8,32,4608]{2,1,0:T(8,128)(2,1)}, bf16[8,32,4608]{2,1,0:T(8,128)(2,1)}, bf16[8,32,2048]{2,1,0:T(8,...) custom-call(bf16[128,4608]{1,0:T(8,128)(2,1)} %get-tuple-element.45.refs_0_, bf16[128,1024]{1,0:T(8,128)(2,1)} %copy-done.2, ...), custom_call_target="tpu_custom_call" | custom-call | tf_op jit(solution)/shard_map/sum_grads/pallas_call | solution.py:589
  398.4 7.5 %bitcast_convert_fusion.1 = (f32[256,4608]{1,0:T(8,128)}, f32[256,4608]{1,0:T(8,128)}) fusion(bf16[8,32,4608]{2,1,0:T(8,128)(2,1)} %get-tuple-element.34, bf16[8,32,4608]{2,1,0:T(8,128)(2,1)} %get-tuple-element.33), kind=kLoop, calls=%fused_computation.1 | loop fusion | flops 2359296 | bytes 14155776 | tf_op jit(solution)/shard_map/convert_element_type | solution.py:614
  405.9 2.9 bitcast_convert_fusion
  409.1 1.0 fusion.41
  410.2 1.0 split.12
  411.2 1.1 bitcast_convert_fusion.4
  412.4 0.6 fusion.42
  413.7 1.0 fusion.14
  414.7 5.8 %fusion.2 = bf16[128,1024]{1,0:T(8,128)(2,1)} fusion(f32[128,1024]{1,0:T(8,128)S(1)} %get-tuple-element.77, bf16[128,4608]{1,0:T(8,128)(2,1)S(1)} %copy-done, bf16[4608,1024]{1,0:T(8,128)(2,1)} %bitcast.146), kind=kOutput, calls=%fused_computation.14 | convolution fusion | flops 1208221696 | bytes 11403264 | tf_op jit(solution)/shard_map/dot_general | solution.py:23
  (186 shorter events, 6.0 us)
Async XLA Ops:
  2.0 84.2 %copy-start.9 = (bf16[128,1024]{1,0:T(8,128)(2,1)S(1)}, bf16[128,1024]{1,0:T(8,128)(2,1)}, u32[]{:S(2)}) copy-start(bf16[128,1024]{1,0:T(8,128)(2,1)} %param.14) | copy-start | bytes 786436
  86.3 3.4 copy-start.54
  86.5 3.2 copy-start.16
  86.8 3.4 copy-start.56
  89.9 2.1 copy-start.7
  91.5 2.0 copy-start.33
  91.8 1.8 copy-start.39
  92.2 1.8 copy-start.30
  93.7 2.6 copy-start.47
  94.0 2.3 copy-start.14
  96.3 6.8 %slice-start.3 = ((s8[9437184]{0:T(1024)(128)(4,1)}), s8[4194304]{0:T(1024)(128)(4,1)S(1)}, s32[]{:S(2)}) async-start(s8[9437184]{0:T(1024)(128)(4,1)} %bitcast.142), calls=%async_computation.3 | async-start | bytes 8388608
  96.5 6.7 %copy-start.2 = (bf16[128,1024]{1,0:T(8,128)(2,1)}, bf16[128,1024]{1,0:T(8,128)(2,1)S(1)}, u32[]{:S(2)}) copy-start(bf16[128,1024]{1,0:T(8,128)(2,1)S(1)} %multiply_convert_fusion.5.refs_1_) | copy-start | bytes 786436
  96.5 6.7 %slice-start.4 = ((s8[9437184]{0:T(1024)(128)(4,1)}), s8[4194304]{0:T(1024)(128)(4,1)S(1)}, s32[]{:S(2)}) async-start(s8[9437184]{0:T(1024)(128)(4,1)} %bitcast.142), calls=%async_computation.4 | async-start | bytes 8388608
  96.5 6.7 %slice-start.5 = ((s8[9437184]{0:T(1024)(128)(4,1)}), s8[1048576]{0:T(1024)(128)(4,1)S(1)}, s32[]{:S(2)}) async-start(s8[9437184]{0:T(1024)(128)(4,1)} %bitcast.142), calls=%async_computation.5 | async-start | bytes 2097152
  103.2 2.9 copy-start.57
  103.2 2.9 copy-start.19
  103.2 20.5 %slice-start = ((s8[9437184]{0:T(1024)(128)(4,1)}), s8[4194304]{0:T(1024)(128)(4,1)S(1)}, s32[]{:S(2)}) async-start(s8[9437184]{0:T(1024)(128)(4,1)} %bitcast.138), calls=%async_computation | async-start | bytes 8388608
  106.2 9.9 %copy-start.20 = (bf16[128,1024]{1,0:T(8,128)(2,1)}, bf16[128,1024]{1,0:T(8,128)(2,1)S(1)}, u32[]{:S(2)}) copy-start(bf16[128,1024]{1,0:T(8,128)(2,1)S(1)} %fusion.18.refs_4_) | copy-start | bytes 786436
  106.2 17.5 %slice-start.1 = ((s8[9437184]{0:T(1024)(128)(4,1)}), s8[4194304]{0:T(1024)(128)(4,1)S(1)}, s32[]{:S(2)}) async-start(s8[9437184]{0:T(1024)(128)(4,1)} %bitcast.138), calls=%async_computation.1 | async-start | bytes 8388608
  106.2 17.5 %slice-start.2 = ((s8[9437184]{0:T(1024)(128)(4,1)}), s8[1048576]{0:T(1024)(128)(4,1)S(1)}, s32[]{:S(2)}) async-start(s8[9437184]{0:T(1024)(128)(4,1)} %bitcast.138), calls=%async_computation.2 | async-start | bytes 2097152
  116.1 7.6 %copy-start.6 = (bf16[128,4608]{1,0:T(8,128)(2,1)}, bf16[128,4608]{1,0:T(8,128)(2,1)S(1)}, u32[]{:S(2)}) copy-start(bf16[128,4608]{1,0:T(8,128)(2,1)S(1)} %get-tuple-element.44.refs_5_) | copy-start | bytes 3538948
  116.1 7.6 %copy-start.3 = (bf16[128,4608]{1,0:T(8,128)(2,1)}, bf16[128,4608]{1,0:T(8,128)(2,1)S(1)}, u32[]{:S(2)}) copy-start(bf16[128,4608]{1,0:T(8,128)(2,1)S(1)} %get-tuple-element.43.refs_6_) | copy-start | bytes 3538948
  127.7 1.8 copy-start.1
  132.1 1.7 copy-start.13
  132.1 1.7 copy-start.34
  134.2 4.1 copy-start.41
  136.2 10.5 %copy-start.5 = (bf16[8,2,128,128]{2,3,1,0:T(8,128)(2,1)S(1)}, bf16[8,2,128,128]{2,3,1,0:T(8,128)(2,1)}, u32[]{:S(2)}) copy-start(bf16[8,2,128,128]{2,3,1,0:T(8,128)(2,1)} %copy-done.4) | copy-start | bytes 1572868
  136.2 10.5 %copy-start.24 = (bf16[1,128,16,32]{1,3,2,0:T(8,128)(2,1)S(1)}, bf16[1,128,16,32]{1,3,2,0:T(8,128)(2,1)}, u32[]{:S(2)}) copy-start(bf16[1,128,16,32]{1,3,2,0:T(8,128)(2,1)} %copy-done.23) | copy-start | bytes 393220
  139.2 7.9 %copy-start.8 = (f32[128,512]{0,1:T(8,128)S(1)}, f32[128,512]{0,1:T(8,128)}, u32[]{:S(2)}) copy-start(f32[128,512]{0,1:T(8,128)} %copy-done.7) | copy-start | bytes 786436
  143.9 2.9 copy-start.26
  143.9 3.2 copy-start.29
  143.9 3.2 copy-start.43
  143.9 3.3 copy-start.53
  147.0 10.3 %copy-start.32 = (pred[128,128]{0,1:T(8,128)(4,1)S(1)}, pred[128,128]{0,1:T(8,128)(4,1)}, u32[]{:S(2)}) copy-start(pred[128,128]{0,1:T(8,128)(4,1)} %copy-done.30) | copy-start | bytes 49156
  147.0 10.3 %copy-start.38 = (f32[8,2,128]{2,1,0:T(2,128)S(1)}, f32[8,2,128]{2,1,0:T(2,128)}, u32[]{:S(2)}) copy-start(f32[8,2,128]{2,1,0:T(2,128)} %copy-done.36) | copy-start | bytes 24580
  148.6 10.2 %copy-start.10 = (bf16[128,1024]{1,0:T(8,128)(2,1)S(1)}, bf16[128,1024]{1,0:T(8,128)(2,1)}, u32[]{:S(2)}) copy-start(bf16[128,1024]{1,0:T(8,128)(2,1)} %param.14) | copy-start | bytes 786436
  148.6 10.2 %copy-start.21 = (bf16[128,1024]{1,0:T(8,128)(2,1)S(1)}, bf16[128,1024]{1,0:T(8,128)(2,1)}, u32[]{:S(2)}) copy-start(bf16[128,1024]{1,0:T(8,128)(2,1)} %get-tuple-element.49) | copy-start | bytes 786436
  148.6 10.2 %copy-start.45 = (f32[1,2,4,128]{3,1,2,0:T(2,128)S(1)}, f32[1,2,4,128]{3,1,2,0:T(2,128)}, u32[]{:S(2)}) copy-start(f32[1,2,4,128]{3,1,2,0:T(2,128)} %copy-done.44) | copy-start | bytes 12292
  148.6 10.2 %copy-start.55 = (f32[128]{0:T(128)S(1)}, f32[128]{0:T(128)}, u32[]{:S(2)}) copy-start(f32[128]{0:T(128)} %copy-done.54) | copy-start | bytes 1540
  158.8 3.9 copy-start.46
  158.8 4.3 %copy-start.51 = (bf16[1024]{0:T(1024)(128)(2,1)S(1)}, bf16[1024]{0:T(1024)(128)(2,1)}, u32[]{:S(2)}) copy-start(bf16[1024]{0:T(1024)(128)(2,1)} %get-tuple-element.37) | copy-start | bytes 6148
  158.8 5.9 %copy-start.15 = (bf16[8,64,2,128]{3,1,2,0:T(8,128)(2,1)S(1)}, bf16[8,64,2,128]{3,1,2,0:T(8,128)(2,1)}, u32[]{:S(2)}) copy-start(bf16[8,64,2,128]{3,1,2,0:T(8,128)(2,1)} %copy-done.14) | copy-start | bytes 786436
  398.4 7.5 %copy-start.11 = (bf16[9,4,32,1024]{3,2,1,0:T(8,128)(2,1)S(1)}, bf16[9,4,32,1024]{3,2,1,0:T(8,128)(2,1)}, u32[]{:S(2)}) copy-start(bf16[9,4,32,1024]{3,2,1,0:T(8,128)(2,1)} %get-tuple-element.35) | copy-start | bytes 7077892
  405.9 2.9 copy-start.18
  409.1 2.1 copy-start.22
  410.2 2.2 copy-start.48
  410.2 3.5 copy-start.17
  410.2 4.5 %copy-start = (bf16[128,4608]{1,0:T(8,128)(2,1)S(1)}, bf16[128,4608]{1,0:T(8,128)(2,1)}, u32[]{:S(2)}) copy-start(bf16[128,4608]{1,0:T(8,128)(2,1)} %get-tuple-element.45.refs_0_) | copy-start | bytes 3538948
  (16 other events, 17.8 us)

commit v4 on v3

--- a/solution.py
+++ b/solution.py
@@ -76,18 +76,6 @@
     return jnp.concatenate(
         [part_one * cos_tab + part_two * sin_tab, part_two * cos_tab - part_one * sin_tab], axis=-1
     )
-
-
-def attn_probs_of(query_bf, key_bf, key_mask, log_total, score_scale):
-    scores = (
-        jnp.einsum("gqkrd,gskd->gkrqs", query_bf, key_bf, preferred_element_type=jnp.float32)
-        * score_scale
-    )
-    if log_total is None:
-        log_total = jnp.log(
-            jnp.sum(jnp.where(key_mask, jnp.exp(scores), 0.0), axis=-1, keepdims=True)
-        )
-    return (jnp.where(key_mask, jnp.exp(scores - log_total), 0.0), log_total)
 
 
 def bit_count(size):
@@ -653,35 +641,42 @@
 
     doc_rows = doc_ids[None, :]
     allowed, positions = doc_tables(doc_rows)
-    key_mask = allowed[:, None, None]
-    cos_tab, sin_tab = rope_tables(positions, HEAD_DIM)
+    key_mask = allowed
+    cos_tab, sin_tab = (t.reshape(1, tok_rows, -1) for t in rope_tables(positions, HEAD_DIM))
+
+    def by_head(values):
+        return values.reshape(tok_rows, -1, HEAD_DIM).transpose(1, 0, 2)
+
+    def by_token(values):
+        return values.transpose(1, 0, 2).reshape(tok_rows, -1)
+
+    def batched(spec, left, right):
+        return jnp.einsum(spec, left, right, preferred_element_type=jnp.float32)
+
     resid_in = tokens.astype(jnp.float32)
     normed_in, unit_in, rms_in = norm_rows(resid_in, full_gattn)
     normed_bf = normed_in.astype(jnp.bfloat16)
     qkv = matmul(normed_bf, qkv_set)
-    query_raw = qkv[:, :q_width].reshape(1, tok_rows, QH, HEAD_DIM)
-    key_raw = qkv[:, q_width : q_width + k_width].reshape(1, tok_rows, KVH, HEAD_DIM)
-    value_bf = qkv[:, q_width + k_width :].astype(jnp.bfloat16).reshape(1, tok_rows, KVH, HEAD_DIM)
+    query_raw = by_head(qkv[:, :q_width])
+    key_raw = by_head(qkv[:, q_width : q_width + k_width])
+    value_bf = by_head(qkv[:, q_width + k_width :].astype(jnp.bfloat16))
     query_normed, query_unit, query_rms = norm_rows(query_raw, full_gquery)
     key_normed, key_unit, key_rms = norm_rows(key_raw, full_gkey)
-    query_bf = (
-        rotate(query_normed, cos_tab, sin_tab)
-        .astype(jnp.bfloat16)
-        .reshape(1, tok_rows, KVH, head_share, HEAD_DIM)
-    )
+    shared = (KVH, head_share * tok_rows, -1)
+    query_bf = rotate(query_normed, cos_tab, sin_tab).astype(jnp.bfloat16).reshape(shared)
     key_bf = rotate(key_normed, cos_tab, sin_tab).astype(jnp.bfloat16)
-    attn_probs, log_total = attn_probs_of(query_bf, key_bf, key_mask, None, score_scale)
-    probs_bf = attn_probs.astype(jnp.bfloat16)
-    mixed_bf = (
-        jnp.einsum("gkrqs,gskd->gqkrd", probs_bf, value_bf, preferred_element_type=jnp.float32)
-        .astype(jnp.bfloat16)
-        .reshape(tok_rows, QH * HEAD_DIM)
-    )
+    scores = batched("kmd,ksd->kms", query_bf, key_bf).reshape(QH, tok_rows, -1) * score_scale
+    log_total = jnp.log(jnp.sum(jnp.where(key_mask, jnp.exp(scores), 0.0), axis=-1, keepdims=True))
+    attn_probs = jnp.where(key_mask, jnp.exp(scores - log_total), 0.0)
+    probs_bf = attn_probs.astype(jnp.bfloat16).reshape(shared)
+    mixed = batched("kms,ksd->kmd", probs_bf, value_bf).astype(jnp.bfloat16)
+    mixed_bf = by_token(mixed.reshape(QH, tok_rows, -1))
     resid_mid = resid_in + matmul(mixed_bf, out_set)
     normed_mid, unit_mid, rms_mid = norm_rows(resid_mid, full_gffn)
     hidden_in = normed_mid.astype(jnp.bfloat16)
     gate_proj = matmul(hidden_in, gate_set)
     up_proj = matmul(hidden_in, up_set)
+    gate_proj, up_proj = lax.optimization_barrier((gate_proj, up_proj))
     gate_sig = jax.nn.sigmoid(gate_proj)
     gate_act = gate_proj * gate_sig
     hidden_bf = (gate_act * up_proj).astype(jnp.bfloat16)
@@ -691,7 +686,7 @@
     grad_y_bf = grad_y.astype(jnp.bfloat16)
     block_out = (resid_mid + matmul(hidden_bf, down_set)).astype(jnp.bfloat16)
 
-    grad_hidden = matmul_t(grad_y_bf, down_set)
+    grad_hidden = lax.optimization_barrier(matmul_t(grad_y_bf, down_set))
     grad_gate_bf = (grad_hidden * up_proj * gate_sig * (1.0 + gate_proj * (1.0 - gate_sig))).astype(
         jnp.bfloat16
     )
@@ -700,35 +695,21 @@
     back_mid, part_gffn = norm_back(grad_norm_mid, unit_mid, rms_mid, full_gffn)
     grad_mid = grad_y + back_mid
     grad_mid_bf = grad_mid.astype(jnp.bfloat16)
-    grad_mixed_bf = (
-        matmul_t(grad_mid_bf, out_set)
-        .astype(jnp.bfloat16)
-        .reshape(1, tok_rows, KVH, head_share, HEAD_DIM)
-    )
-    grad_scores = jnp.einsum(
-        "gqkrd,gskd->gkrqs", grad_mixed_bf, value_bf, preferred_element_type=jnp.float32
-    )
-    grad_value_bf = (
-        jnp.einsum("gkrqs,gqkrd->gskd", probs_bf, grad_mixed_bf, preferred_element_type=jnp.float32)
-        .astype(jnp.bfloat16)
-        .reshape(tok_rows, KVH * HEAD_DIM)
-    )
+    grad_mixed_bf = by_head(matmul_t(grad_mid_bf, out_set).astype(jnp.bfloat16)).reshape(shared)
+    grad_scores = batched("kmd,ksd->kms", grad_mixed_bf, value_bf).reshape(attn_probs.shape)
+    grad_value_bf = by_token(batched("kms,kmd->ksd", probs_bf, grad_mixed_bf).astype(jnp.bfloat16))
     row_dot = jnp.sum(attn_probs * grad_scores, axis=-1, keepdims=True)
-    grad_logits = (attn_probs * (grad_scores - row_dot) * score_scale).astype(jnp.bfloat16)
-    grad_query_rot = jnp.einsum(
-        "gkrqs,gskd->gqkrd", grad_logits, key_bf, preferred_element_type=jnp.float32
-    ).reshape(1, tok_rows, QH, HEAD_DIM)
-    grad_key_rot = jnp.einsum(
-        "gkrqs,gqkrd->gskd", grad_logits, query_bf, preferred_element_type=jnp.float32
-    )
+    grad_logits = (attn_probs * (grad_scores - row_dot) * score_scale).astype(jnp.bfloat16).reshape(shared)
+    grad_query_rot = batched("kms,ksd->kmd", grad_logits, key_bf).reshape(query_raw.shape)
+    grad_key_rot = batched("kms,kmd->ksd", grad_logits, query_bf)
     grad_query_raw, part_gquery = norm_back(
         rotate_back(grad_query_rot, cos_tab, sin_tab), query_unit, query_rms, full_gquery
     )
     grad_key_raw, part_gkey = norm_back(
         rotate_back(grad_key_rot, cos_tab, sin_tab), key_unit, key_rms, full_gkey
     )
-    grad_query_bf = grad_query_raw.astype(jnp.bfloat16).reshape(tok_rows, QH * HEAD_DIM)
-    grad_key_bf = grad_key_raw.astype(jnp.bfloat16).reshape(tok_rows, KVH * HEAD_DIM)
+    grad_query_bf = by_token(grad_query_raw.astype(jnp.bfloat16))
+    grad_key_bf = by_token(grad_key_raw.astype(jnp.bfloat16))
     grad_qkv_bf = jnp.concatenate([grad_query_bf, grad_key_bf, grad_value_bf], axis=1)
     grad_norm_in = matmul_t(grad_qkv_bf, qkv_set)
     back_in, part_gattn = norm_back(grad_norm_in, unit_in, rms_in, full_gattn)

time: 421 us -> 413 us (0.981)
  local copies, waits for them, and re-layouts: 25.9 us -> 19.6 us
    mul x12 -> x0, local copies, waits for them, and re-layouts: 13 us -> none  [the longest x4 6.09 us: norm_rows(): normed = values * inv_rms]
    dot_general x5, matrix products: 26.7 us -> 16.8 us  [matmul_t(): lax.dot_general(left, right, (((1,), (1,)), ((), ())), preferred_element_...]
    dot_general x6, matrix products: 4.62 us -> 11.6 us  [batched(): return jnp.einsum(spec, left, right, preferred_element_type=jnp.float32)]
    convert_element_type x0 -> x3, other arithmetic: none -> 6.12 us  [the longest x1 5.84 us: local(): grad_up_bf = (grad_hidden * gate_act).astype(jnp.bfloat16)]
where the time goes in v4:
time: 413 us
  Pallas kernels  316 us (77%)
  matrix products  48.2 us (12%)
  other arithmetic  27.5 us (7%)
  local copies, waits for them, and re-layouts  19.6 us (5%)
    pallas_call x1, Pallas kernels, reduce_grads(): pl.pallas_call(functools.partial(sum_kernel, cfg), name='sum_grads', out_...  233 us
    pallas_call x1, Pallas kernels, gather_all(): pl.pallas_call(functools.partial(gather_kernel, {'items': items, 'n_in':...  82.9 us
    dot_general x5, matrix products, matmul(): return jnp.dot(left, right, preferred_element_type=jnp.float32)  19.7 us
    dot_general x5, matrix products, matmul_t(): lax.dot_general(left, right, (((1,), (1,)), ((), ())), preferred_element_...  16.8 us
    convert_element_type x4, other arithmetic, reduce_grads(): v.reshape(-1, v.shape[-1]).astype(jnp.float32)  11.8 us
    dot_general x6, matrix products, batched(): return jnp.einsum(spec, left, right, preferred_element_type=jnp.float32)  11.6 us

profile of v4, /device:TPU:0, one launch (start us, length us, event | category | flops | bytes accessed | tf_op | source)
XLA Modules:
  0.0 412.6 jit_solution(5266421755350442721)
XLA Ops:
  0.6 1.4 fusion.48.refs_7_
  2.0 82.9 %gather_weights.1 = (bf16[4,256,2048]{2,1,0:T(8,128)(2,1)}, bf16[4,256,1024]{2,1,0:T(8,128)(2,1)}, bf16[4,256,4608]{2,1,0:T(8,128)(2,1)}, bf16[4,256,4608]{2,1,0...) custom-call(bf16[256,1024]{1,0:T(8,128)(2,1)} %refs_0_.1, bf16[256,512]{1,0:T(8,128)(2,1)} %refs_1_.1, ...), custom_call_target="tpu_custom_call" | custom-call | tf_op jit(solution)/shard_map/gather_weights/pallas_call | solution.py:256
  85.0 0.7 copy.109
  85.7 0.6 convert_bitcast_fusion
  86.9 2.9 fusion.65
  92.1 0.5 copy-done.39
  92.8 0.6 copy-done.27
  93.4 1.3 convolution_multiply_fusion
  94.7 1.1 slice.130
  96.0 0.8 fusion.39
  97.3 3.0 convolution_convert_fusion
  100.2 1.1 copy.73
  101.3 0.8 reshape.440
  102.1 1.0 copy.74
  103.2 1.6 multiply_reduce_fusion.5
  105.0 6.7 %fusion.67 = f32[128,4608]{1,0:T(8,128)} fusion(bf16[128,1024]{1,0:T(8,128)(2,1)S(1)} %multiply_convert_fusion.4.refs_1_, bf16[1024,4608]{1,0:T(8,128)(2,1)} %bitcast.111), kind=kOutput, calls=%fused_computation.140 | convolution fusion | flops 1207959552 | bytes 12058624 | tf_op jit(solution)/shard_map/dot_general | solution.py:23
  111.7 2.8 fusion.66
  114.7 0.7 copy-done.10
  115.4 0.8 slice-done.1
  116.4 4.6 %fusion.68 = f32[128,4608]{1,0:T(8,128)} fusion(bf16[128,1024]{1,0:T(8,128)(2,1)S(1)} %fusion.30.refs_4_, bf16[4608,1024]{1,0:T(8,128)(2,1)S(1)} %bitcast.110), kind=kOutput, calls=%fused_computation.141 | convolution fusion | flops 1207959552 | bytes 12058624 | tf_op jit(solution)/shard_map/dot_general | solution.py:27
  121.0 5.8 %multiply_convert_fusion = (bf16[128,4608]{1,0:T(8,128)(2,1)S(1)}, bf16[128,4608]{1,0:T(8,128)(2,1)S(1)}, bf16[128,4608]{1,0:T(8,128)(2,1)}) fusion(f32[128,4608]{1,0:T(8,128)} %fusion.68, f32[128,4608]{1,0:T(8,128)} %fusion.66, f32[128,4608]{1,0:T(8,128)} %fusion.67), kind=kLoop, calls=%fused_computation.5 | loop fusion | flops 8847360 | bytes 10616832 | tf_op jit(solution)/shard_map/convert_element_type | solution.py:693
  126.9 3.1 fusion.69
  130.0 3.7 multiply_reduce_fusion.2
  133.7 1.0 fusion.61
  134.7 0.7 copy-done.11
  135.4 1.5 convolution_convert_fusion.1
  137.0 1.2 copy.75
  138.5 1.3 fusion.37
  139.8 1.4 fusion.9
  141.2 2.7 fusion.14
  144.0 1.1 copy.79
  145.1 1.1 reshape.448
  147.2 2.7 fusion.13
  150.4 0.6 convolution_convert_fusion.2
  151.2 3.8 fusion.28
  155.4 0.6 bitcast_convert_fusion.5.refs_9_
  156.0 0.8 pad_maximum_fusion.1.refs_7_
  156.9 0.8 copy.88.refs_3_
  157.7 232.8 %sum_grads.1 = (bf16[9,4,32,1024]{3,2,1,0:T(8,128)(2,1)}, bf16[8,32,4608]{2,1,0:T(8,128)(2,1)}, bf16[8,32,4608]{2,1,0:T(8,128)(2,1)}, bf16[8,32,2048]{2,1,0:T(8,...) custom-call(bf16[128,4608]{1,0:T(8,128)(2,1)} %get-tuple-element.53.refs_0_, bf16[128,1024]{1,0:T(8,128)(2,1)} %copy-done.4, ...), custom_call_target="tpu_custom_call" | custom-call | tf_op jit(solution)/shard_map/sum_grads/pallas_call | solution.py:577
  390.5 7.5 %bitcast_convert_fusion.1 = (f32[256,4608]{1,0:T(8,128)}, f32[256,4608]{1,0:T(8,128)}) fusion(bf16[8,32,4608]{2,1,0:T(8,128)(2,1)} %get-tuple-element.38, bf16[8,32,4608]{2,1,0:T(8,128)(2,1)} %get-tuple-element.37), kind=kLoop, calls=%fused_computation.3 | loop fusion | flops 2359296 | bytes 14155776 | tf_op jit(solution)/shard_map/convert_element_type | solution.py:602
  398.0 2.9 bitcast_convert_fusion
  401.2 1.0 fusion.62
  402.3 1.0 split.12
  403.3 1.1 bitcast_convert_fusion.4
  404.5 0.6 fusion.64
  405.2 0.6 dynamic-slice_bitcast_fusion
  405.8 1.0 fusion.27
  406.8 5.8 %fusion.11 = bf16[128,1024]{1,0:T(8,128)(2,1)} fusion(f32[128,1024]{1,0:T(8,128)S(1)} %get-tuple-element.77, bf16[128,4608]{1,0:T(8,128)(2,1)S(1)} %copy-done, bf16[4608,1024]{1,0:T(8,128)(2,1)} %bitcast.107), kind=kOutput, calls=%fused_computation.22 | convolution fusion | flops 1208221696 | bytes 11403264 | tf_op jit(solution)/shard_map/dot_general | solution.py:23
  (169 shorter events, 6.5 us)
Async XLA Ops:
  2.0 84.3 %copy-start.6 = (bf16[128,1024]{1,0:T(8,128)(2,1)S(1)}, bf16[128,1024]{1,0:T(8,128)(2,1)}, u32[]{:S(2)}) copy-start(bf16[128,1024]{1,0:T(8,128)(2,1)} %param.14) | copy-start | bytes 786436
  86.6 3.3 copy-start.16
  89.9 1.5 copy-start.8
  89.9 0.7 copy-start.44
  90.2 0.7 copy-start.29
  90.9 1.9 copy-start.25
  91.3 4.7 %copy-start.22 = (bf16[8,256,64]{1,2,0:T(8,128)(2,1)}, bf16[8,256,64]{1,2,0:T(8,128)(2,1)S(1)}, u32[]{:S(2)}) copy-start(bf16[8,256,64]{1,2,0:T(8,128)(2,1)S(1)} %copy_dynamic-update-slice_fusion) | copy-start | bytes 786436
  94.7 8.4 %copy-start.3 = (bf16[4,256,1024]{2,1,0:T(8,128)(2,1)S(1)}, bf16[4,256,1024]{2,1,0:T(8,128)(2,1)}, u32[]{:S(2)}) copy-start(bf16[4,256,1024]{2,1,0:T(8,128)(2,1)} %get-tuple-element.29) | copy-start | bytes 6291460
  97.3 5.9 %copy-start.12 = (pred[8,256,128]{1,2,0:T(32,128)(4,1)}, pred[8,256,128]{1,2,0:T(32,128)(4,1)S(1)}, u32[]{:S(2)}) copy-start(pred[8,256,128]{1,2,0:T(32,128)(4,1)S(1)} %copy.70) | copy-start | bytes 786436
  102.1 2.7 copy-start.35
  103.2 1.6 copy-start.14
  104.8 6.8 %slice-start.6 = ((s8[9437184]{0:T(1024)(128)(4,1)}), s8[4194304]{0:T(1024)(128)(4,1)S(1)}, s32[]{:S(2)}) async-start(s8[9437184]{0:T(1024)(128)(4,1)} %bitcast.115), calls=%async_computation.6 | async-start | bytes 8388608
  104.9 6.7 %copy-start.4 = (bf16[128,1024]{1,0:T(8,128)(2,1)}, bf16[128,1024]{1,0:T(8,128)(2,1)S(1)}, u32[]{:S(2)}) copy-start(bf16[128,1024]{1,0:T(8,128)(2,1)S(1)} %multiply_convert_fusion.4.refs_1_) | copy-start | bytes 786436
  105.0 6.7 %slice-start.7 = ((s8[9437184]{0:T(1024)(128)(4,1)}), s8[4194304]{0:T(1024)(128)(4,1)S(1)}, s32[]{:S(2)}) async-start(s8[9437184]{0:T(1024)(128)(4,1)} %bitcast.115), calls=%async_computation.7 | async-start | bytes 8388608
  105.0 6.7 %slice-start.8 = ((s8[9437184]{0:T(1024)(128)(4,1)}), s8[1048576]{0:T(1024)(128)(4,1)S(1)}, s32[]{:S(2)}) async-start(s8[9437184]{0:T(1024)(128)(4,1)} %bitcast.115), calls=%async_computation.8 | async-start | bytes 2097152
  111.6 3.7 slice-start
  111.7 2.9 copy-start.45
  111.7 2.9 copy-start.19
  111.7 4.4 %slice-start.1 = ((s8[9437184]{0:T(1024)(128)(4,1)}), s8[4194304]{0:T(1024)(128)(4,1)S(1)}, s32[]{:S(2)}) async-start(s8[9437184]{0:T(1024)(128)(4,1)} %bitcast.108), calls=%async_computation.1 | async-start | bytes 8388608
  111.7 4.7 %slice-start.2 = ((s8[9437184]{0:T(1024)(128)(4,1)}), s8[1048576]{0:T(1024)(128)(4,1)S(1)}, s32[]{:S(2)}) async-start(s8[9437184]{0:T(1024)(128)(4,1)} %bitcast.108), calls=%async_computation.2 | async-start | bytes 2097152
  114.7 0.7 copy-start.10
  121.0 9.0 %slice-start.3 = ((s8[9437184]{0:T(1024)(128)(4,1)}), s8[4194304]{0:T(1024)(128)(4,1)S(1)}, s32[]{:S(2)}) async-start(s8[9437184]{0:T(1024)(128)(4,1)} %bitcast.112), calls=%async_computation.3 | async-start | bytes 8388608
  121.0 9.0 %slice-start.4 = ((s8[9437184]{0:T(1024)(128)(4,1)}), s8[4194304]{0:T(1024)(128)(4,1)S(1)}, s32[]{:S(2)}) async-start(s8[9437184]{0:T(1024)(128)(4,1)} %bitcast.112), calls=%async_computation.4 | async-start | bytes 8388608
  126.9 3.1 copy-start.2
  126.9 3.1 copy-start.1
  126.9 3.1 slice-start.5
  134.7 0.7 copy-start.11
  137.0 2.8 copy-start.5
  137.0 2.8 copy-start.13
  138.5 5.5 %copy-start.20 = (bf16[8,256,64]{1,0,2:T(8,128)(2,1)}, bf16[8,256,64]{1,0,2:T(8,128)(2,1)S(1)}, u32[]{:S(2)}) copy-start(bf16[8,256,64]{1,0,2:T(8,128)(2,1)S(1)} %reshape.447) | copy-start | bytes 786436
  141.2 5.0 %copy-start.26 = (f32[128,32]{0,1:T(8,128)S(1)}, f32[128,32]{0,1:T(8,128)}, u32[]{:S(2)}) copy-start(f32[128,32]{0,1:T(8,128)} %copy-done.25) | copy-start | bytes 49156
  144.0 2.4 copy-start.30
  144.0 2.4 copy-start.38
  146.2 1.0 copy-start.23
  146.6 3.3 copy-start.32
  146.6 3.3 copy-start.40
  146.8 3.6 copy-start.21
  149.9 1.3 copy-start.7
  149.9 1.2 copy-start.34
  149.9 1.2 copy-start.43
  151.2 4.0 copy-start.41
  151.2 5.7 %copy-start.15 = (bf16[128,16,64]{0,2,1:T(8,128)(2,1)S(1)}, bf16[128,16,64]{0,2,1:T(8,128)(2,1)}, u32[]{:S(2)}) copy-start(bf16[128,16,64]{0,2,1:T(8,128)(2,1)} %copy-done.14) | copy-start | bytes 786436
  390.5 7.5 %copy-start.9 = (bf16[9,4,32,1024]{3,2,1,0:T(8,128)(2,1)S(1)}, bf16[9,4,32,1024]{3,2,1,0:T(8,128)(2,1)}, u32[]{:S(2)}) copy-start(bf16[9,4,32,1024]{3,2,1,0:T(8,128)(2,1)} %get-tuple-element.39) | copy-start | bytes 7077892
  398.0 2.9 copy-start.18
  401.2 2.1 copy-start.24
  402.3 2.2 copy-start.36
  402.3 3.5 copy-start.17
  402.3 4.5 %copy-start = (bf16[128,4608]{1,0:T(8,128)(2,1)S(1)}, bf16[128,4608]{1,0:T(8,128)(2,1)}, u32[]{:S(2)}) copy-start(bf16[128,4608]{1,0:T(8,128)(2,1)} %get-tuple-element.53.refs_0_) | copy-start | bytes 3538948
  (7 other events, 4.0 us)
